TPU v7x, 32 devices: a whole 2x2x4 slice. The times are simulated.
32 devices in a mesh: dp: 4 (over y, core), row: 4 (over z), col: 2 (over x).
Axes of the slice: x: 2, y: 2, z: 4, core: 2. Of those that a mesh axis runs over, the one named last changes fastest.
Arguments:
- inputs: bfloat16 [4096, 1024], P(('dp', 'col'), 'row'), may hold values from -6 to 6
- cotangent: bfloat16 [4096, 1024], P(('dp', 'col'), 'row'), may hold values from -6 to 6
- seg_parent: int32 [52], P('dp'), may hold values from 0 to 51, as said below
- token_depth: int32 [4096], P('dp'), may hold values from 0 to 383, as said below
- ln1_gain: float32 [1024], P('row'), may hold values from 0.25 to 1.75
- ln1_bias: float32 [1024], P('row'), may hold values from -1.5 to 1.5
- w_qkv: bfloat16 [1024, 3, 1024], P('row', None, 'col'), may hold values from -0.1875 to 0.1875
- b_qv: float32 [2, 1024], P(None, 'col'), may hold values from -1.5 to 1.5
- w_out: bfloat16 [1024, 1024], P('col', 'row'), may hold values from -0.5 to 0.5
- b_out: float32 [1024], P('row'), may hold values from -1.5 to 1.5
- ln2_gain: float32 [1024], P('row'), may hold values from 0.25 to 1.75
- ln2_bias: float32 [1024], P('row'), may hold values from -1.5 to 1.5
- w_up: bfloat16 [1024, 4096], P('row', 'col'), may hold values from -0.1875 to 0.1875
- b_up: float32 [4096], P('col'), may hold values from -1.5 to 1.5
- w_down: bfloat16 [4096, 1024], P('col', 'row'), may hold values from -0.125 to 0.125
- b_down: float32 [1024], P('row'), may hold values from -1.5 to 1.5
Outputs:
- result: float32 [4096, 1024], P(('dp', 'col'), 'row')
- input_grad: float32 [4096, 1024], P(('dp', 'col'), 'row')
- grad_ln1_gain: float32 [1024], P('row')
- grad_ln1_bias: float32 [1024], P('row')
- grad_w_qkv: float32 [1024, 3, 1024], P('row', None, 'col')
- grad_b_qv: float32 [2, 1024], P(None, 'col')
- grad_w_out: float32 [1024, 1024], P('col', 'row')
- grad_b_out: float32 [1024], P('row')
- grad_ln2_gain: float32 [1024], P('row')
- grad_ln2_bias: float32 [1024], P('row')
- grad_w_up: float32 [1024, 4096], P('row', 'col')
- grad_b_up: float32 [4096], P('col')
- grad_w_down: float32 [4096, 1024], P('col', 'row')
- grad_b_down: float32 [1024], P('row')
Inputs may be any that keep to these rules, and one draw needn't show every extreme that they name: `seg_parent`: tree t holds tokens t * 1024 to (t + 1) * 1024 - 1 and segments 13 t to 13 t + 12, laid out as segment(i) says: segment 13 t is the trunk of 256 tokens and is its own parent; four of the other twelve are branches with the trunk as parent, eight are leaves, two for every branch, with that branch as parent; segment 13 t + 12 is a branch; which ids play the other parts is drawn. `token_depth`: the token at offset j of its segment has depth j in a trunk, 256 + j in a branch and 320 + j in a leaf.
All inputs are finite; a program needn't handle non-finite values.
Results may differ from a plain program's by a relative error of at most 0.011.
Values may be sent and summed in bfloat16 or wider, within the bound.
A program may use at most 192 MiB of HBM per device.

v0:
```python
import math

import jax
import jax.numpy as jnp
from jax import lax
from jax.sharding import PartitionSpec as P

HD = 128


EPS = 1e-05
MASKED = -1e30


def gelu_value(values):
    return 0.5 * values * (1.0 + jax.scipy.special.erf(values / math.sqrt(2.0)))


def gelu_slope(values):
    return 0.5 * (1.0 + jax.scipy.special.erf(values / math.sqrt(2.0))) + values * jnp.exp(
        -0.5 * values * values
    ) / math.sqrt(2.0 * math.pi)


def width_sums(first_term, second_term):
    return lax.psum((jnp.sum(first_term, axis=1), jnp.sum(second_term, axis=1)), "row")


def normalize(values, norm_gain, norm_bias, feature_count):
    row_total, square = width_sums(values, values * values)
    row_mean = row_total / feature_count
    inv_std = lax.rsqrt(square / feature_count - row_mean * row_mean + EPS)
    normed = (values - row_mean[:, None]) * inv_std[:, None]
    return (normed, inv_std, (normed * norm_gain + norm_bias).astype(jnp.bfloat16))


def normalize_back(upstream, normed, inv_std, norm_gain, feature_count):
    spread = upstream * norm_gain
    row_total, cross_sum = width_sums(spread, spread * normed)
    return inv_std[:, None] * (
        spread - row_total[:, None] / feature_count - normed * (cross_sum[:, None] / feature_count)
    )


def contract(left_op, right_op, flipped):
    if flipped:
        return lax.dot_general(
            left_op, right_op, (((1,), (1,)), ((), ())), preferred_element_type=jnp.float32
        )
    return jnp.dot(left_op, right_op, preferred_element_type=jnp.float32)


def outer_sum(left_op, right_op):
    return lax.dot_general(
        left_op, right_op, (((0,), (0,)), ((), ())), preferred_element_type=jnp.float32
    )


def across_rows(operand, weight_block, flipped):
    gathered = lax.all_gather(operand, "col", axis=0, tiled=True)
    row_count = gathered.shape[0] // lax.axis_size("row")

    def partial_term(row_start, row_num):
        return contract(gathered, weight_block, flipped)

    return (
        lax.psum_scatter(
            partial_term(jnp.int32(0), row_count * lax.axis_size("row")),
            "row",
            scatter_dimension=0,
            tiled=True,
        ),
        gathered,
    )


def across_cols(operand, weight_block, flipped):
    gathered = lax.all_gather(operand, "row", axis=0, tiled=True)
    row_count = gathered.shape[0] // lax.axis_size("col")

    def partial_term(row_start, row_num):
        return contract(gathered, weight_block, flipped)

    return (
        lax.psum_scatter(
            partial_term(jnp.int32(0), row_count * lax.axis_size("col")),
            "col",
            scatter_dimension=0,
            tiled=True,
        ),
        gathered,
    )


def tree_labels(seg_parent, token_depth):
    seg_count = seg_parent.shape[0]
    tree_len = token_depth.shape[0]
    seg_len = tree_len // 16
    slot_ids = jnp.arange(seg_count, dtype=jnp.int32)
    where_at = jnp.arange(tree_len, dtype=jnp.int32)
    segment = jnp.where(where_at < 4 * seg_len, 0, 1 + (where_at - 4 * seg_len) // seg_len)
    parent_local = seg_parent - lax.axis_index("dp") * seg_count
    parent_one = jnp.sum(
        jnp.where(segment[:, None] == slot_ids[None, :], parent_local[None, :], 0), axis=1
    )
    parent_two = jnp.sum(
        jnp.where(parent_one[:, None] == slot_ids[None, :], parent_local[None, :], 0), axis=1
    )
    return (segment, parent_one, parent_two, token_depth)


def block_scores(query_block, key_rows, labels, query_start, slopes):
    segment, parent_one, parent_two, token_depth = labels
    block_size = query_block.shape[0]
    query_seg = lax.dynamic_slice_in_dim(segment, query_start, block_size, 0)
    query_one = lax.dynamic_slice_in_dim(parent_one, query_start, block_size, 0)
    query_two = lax.dynamic_slice_in_dim(parent_two, query_start, block_size, 0)
    query_depth = lax.dynamic_slice_in_dim(token_depth, query_start, block_size, 0)
    allowed = (
        (segment[None, :] == query_seg[:, None])
        | (segment[None, :] == query_one[:, None])
        | (segment[None, :] == query_two[:, None])
    ) & (token_depth[None, :] <= query_depth[:, None])
    score_scale = query_block.shape[2] ** (-0.5)
    raw = jnp.einsum("qhd,khd->hqk", query_block, key_rows, preferred_element_type=jnp.float32)
    distance = (query_depth[:, None] - token_depth[None, :]).astype(jnp.float32)
    scores = raw * score_scale - slopes[:, None, None] * distance[None]
    return jnp.where(allowed[None], scores, MASKED)


def attention_forward(queries, key_rows, value_rows, labels, slopes, offset):
    block_size = min(512, queries.shape[0])
    blocks = queries.shape[0] // block_size

    def one_block(block_index):
        block_first = block_index * block_size
        query_block = lax.dynamic_slice_in_dim(queries, block_first, block_size, 0)
        scores = block_scores(query_block, key_rows, labels, offset + block_first, slopes)
        top_score = jnp.max(scores, axis=2, keepdims=True)
        weights = jnp.exp(scores - top_score)
        weight_total = jnp.sum(weights, axis=2, keepdims=True)
        probs = (weights / weight_total).astype(jnp.bfloat16)
        mixed = jnp.einsum("hqk,khd->qhd", probs, value_rows, preferred_element_type=jnp.float32)
        return (mixed, (top_score + jnp.log(weight_total))[:, :, 0])

    return lax.map(one_block, jnp.arange(blocks, dtype=jnp.int32))


def attention_backward(
    queries, key_rows, value_rows, grad_mixed, log_total, labels, slopes, offset
):
    block_size = min(512, queries.shape[0])
    blocks = queries.shape[0] // block_size
    score_scale = queries.shape[2] ** (-0.5)

    def one_block(carry, items):
        key_grad, value_grad = carry
        block_index, block_total = items
        block_first = block_index * block_size
        query_block = lax.dynamic_slice_in_dim(queries, block_first, block_size, 0)
        grad_block = lax.dynamic_slice_in_dim(grad_mixed, block_first, block_size, 0)
        scores = block_scores(query_block, key_rows, labels, offset + block_first, slopes)
        probs = jnp.exp(scores - block_total[:, :, None])
        grad_probs = jnp.einsum(
            "qhd,khd->hqk", grad_block, value_rows, preferred_element_type=jnp.float32
        )
        centre = jnp.sum(probs * grad_probs, axis=2, keepdims=True)
        grad_scores = (probs * (grad_probs - centre)).astype(jnp.bfloat16)
        query_grad = (
            jnp.einsum("hqk,khd->qhd", grad_scores, key_rows, preferred_element_type=jnp.float32)
            * score_scale
        )
        key_grad = (
            key_grad
            + jnp.einsum(
                "hqk,qhd->khd", grad_scores, query_block, preferred_element_type=jnp.float32
            )
            * score_scale
        )
        value_grad = value_grad + jnp.einsum(
            "hqk,qhd->khd",
            probs.astype(jnp.bfloat16),
            grad_block,
            preferred_element_type=jnp.float32,
        )
        return ((key_grad, value_grad), query_grad)

    empty = jnp.zeros(key_rows.shape, jnp.float32)
    (key_grad, value_grad), query_grad = lax.scan(
        one_block, (empty, empty), (jnp.arange(blocks, dtype=jnp.int32), log_total)
    )
    return (key_grad, value_grad, query_grad)


def on_device(
    inputs,
    cotangent,
    seg_parent,
    token_depth,
    ln1_gain,
    ln1_bias,
    w_qkv,
    b_qv,
    w_out,
    b_out,
    ln2_gain,
    ln2_bias,
    w_up,
    b_up,
    w_down,
    b_down,
):
    feature_count = inputs.shape[1] * lax.axis_size("row")
    col_width = w_qkv.shape[2]
    heads_here = col_width // HD
    qkv_flat = w_qkv.reshape(w_qkv.shape[0], 3 * col_width)
    labels = tree_labels(seg_parent, token_depth)
    heads_seen = lax.axis_index("col") * heads_here + jnp.arange(heads_here, dtype=jnp.int32)
    slopes = jnp.exp2(-(heads_seen + 1).astype(jnp.float32))
    states = inputs.astype(jnp.float32)
    normed_one, inv_one, entry_one = normalize(states, ln1_gain, ln1_bias, feature_count)
    projected, entry_one_all = across_rows(entry_one, qkv_flat, False)
    tok_rows = projected.shape[0]
    projected = projected.reshape(tok_rows, 3, col_width)
    queries = (projected[:, 0] + b_qv[0]).astype(jnp.bfloat16)
    keys_here = projected[:, 1].astype(jnp.bfloat16)
    values_here = (projected[:, 2] + b_qv[1]).astype(jnp.bfloat16)
    pair_all = lax.all_gather(
        jnp.stack([keys_here, values_here], axis=1), "row", axis=0, tiled=True
    )
    key_rows = pair_all[:, 0].reshape(-1, heads_here, HD)
    value_rows = pair_all[:, 1].reshape(-1, heads_here, HD)
    query_heads = queries.reshape(tok_rows, heads_here, HD)
    offset = lax.axis_index("row") * tok_rows
    mixed, log_total = attention_forward(query_heads, key_rows, value_rows, labels, slopes, offset)
    mixed = mixed.reshape(tok_rows, col_width).astype(jnp.bfloat16)
    attn_out, mixed_all = across_cols(mixed, w_out, False)
    middle = states + attn_out + b_out
    normed_two, inv_two, entry_two = normalize(middle, ln2_gain, ln2_bias, feature_count)
    hidden_pre, entry_two_all = across_rows(entry_two, w_up, False)
    hidden_pre = hidden_pre + b_up
    hidden = gelu_value(hidden_pre).astype(jnp.bfloat16)
    ffn_out, hidden_all = across_cols(hidden, w_down, False)
    result = middle + ffn_out + b_down
    grad_hidden, down_all = across_rows(cotangent, w_down, True)
    grad_pre = (grad_hidden * gelu_slope(hidden_pre)).astype(jnp.bfloat16)
    grad_entry_two, pre_all = across_cols(grad_pre, w_up, True)
    grad_middle = cotangent.astype(jnp.float32) + normalize_back(
        grad_entry_two, normed_two, inv_two, ln2_gain, feature_count
    )
    grad_branch = grad_middle.astype(jnp.bfloat16)
    grad_mixed, branch_all = across_rows(grad_branch, w_out, True)
    grad_mixed = grad_mixed.astype(jnp.bfloat16).reshape(tok_rows, heads_here, HD)
    key_grad, value_grad, query_grad = attention_backward(
        query_heads, key_rows, value_rows, grad_mixed, log_total, labels, slopes, offset
    )
    kv_grads = lax.psum_scatter(
        jnp.stack([key_grad.reshape(-1, col_width), value_grad.reshape(-1, col_width)], axis=1),
        "row",
        scatter_dimension=0,
        tiled=True,
    )
    grad_projected = jnp.stack(
        [
            query_grad.reshape(tok_rows, col_width).astype(jnp.bfloat16),
            kv_grads[:, 0].astype(jnp.bfloat16),
            kv_grads[:, 1].astype(jnp.bfloat16),
        ],
        axis=1,
    )
    grad_entry_one, proj_all = across_cols(
        grad_projected.reshape(tok_rows, 3 * col_width), qkv_flat, True
    )
    input_grad = grad_middle + normalize_back(
        grad_entry_one, normed_one, inv_one, ln1_gain, feature_count
    )
    proj_sums = jnp.sum(proj_all.astype(jnp.float32), axis=0).reshape(3, col_width)
    weight_terms = (
        outer_sum(entry_one_all, proj_all).reshape(w_qkv.shape),
        jnp.stack([proj_sums[0], proj_sums[2]], axis=0),
        outer_sum(mixed_all, branch_all),
        jnp.sum(branch_all.astype(jnp.float32), axis=0),
        outer_sum(entry_two_all, pre_all),
        jnp.sum(pre_all.astype(jnp.float32), axis=0),
        outer_sum(hidden_all, down_all),
        jnp.sum(down_all.astype(jnp.float32), axis=0),
    )
    (
        grad_w_qkv,
        grad_b_qv,
        grad_w_out,
        grad_b_out,
        grad_w_up,
        grad_b_up,
        grad_w_down,
        grad_b_down,
    ) = lax.psum(
        (
            weight_terms[0],
            weight_terms[1],
            weight_terms[2],
            weight_terms[3],
            weight_terms[4],
            weight_terms[5],
            weight_terms[6],
            weight_terms[7],
        ),
        "dp",
    )
    norm_terms = (
        jnp.sum(grad_entry_one * normed_one, axis=0),
        jnp.sum(grad_entry_one, axis=0),
        jnp.sum(grad_entry_two * normed_two, axis=0),
        jnp.sum(grad_entry_two, axis=0),
    )
    grad_ln1_gain, grad_ln1_bias, grad_ln2_gain, grad_ln2_bias = lax.psum(
        (norm_terms[0], norm_terms[1], norm_terms[2], norm_terms[3]), ("dp", "col")
    )
    return (
        result,
        input_grad,
        grad_ln1_gain,
        grad_ln1_bias,
        grad_w_qkv,
        grad_b_qv,
        grad_w_out,
        grad_b_out,
        grad_ln2_gain,
        grad_ln2_bias,
        grad_w_up,
        grad_b_up,
        grad_w_down,
        grad_b_down,
    )


def solution(mesh):
    placed = (
        P(("dp", "col"), "row"),
        P(("dp", "col"), "row"),
        P("dp"),
        P("dp"),
        P("row"),
        P("row"),
        P("row", None, "col"),
        P(None, "col"),
        P("col", "row"),
        P("row"),
        P("row"),
        P("row"),
        P("row", "col"),
        P("col"),
        P("col", "row"),
        P("row"),
    )
    return jax.shard_map(
        on_device,
        mesh=mesh,
        in_specs=placed,
        out_specs=(
            P(("dp", "col"), "row"),
            P(("dp", "col"), "row"),
            P("row"),
            P("row"),
            P("row", None, "col"),
            P(None, "col"),
            P("col", "row"),
            P("row"),
            P("row"),
            P("row"),
            P("row", "col"),
            P("col"),
            P("col", "row"),
            P("row"),
        ),
        check_vma=False,
    )
```

profile of v0, /device:TPU:0, one launch (start us, length us, event | category | flops | bytes accessed | tf_op | source)
XLA Modules:
  0.0 1127.7 jit_solution(2528115706905828047)
XLA Ops:
  8.5 13.5 %all-reduce.4 = (f32[512]{0:T(512)S(1)}, f32[512]{0:T(512)S(1)}) all-reduce(f32[512]{0:T(512)S(1)} %get-tuple-element.134, f32[512]{0:T(512)S(1)} %get-tuple-element.133), channel_id=1, replica_groups=mesh['dp'=4,'row'=4,'col'=2] {'row'}, use_global_device_ids=true, to_apply=%region_3.4 | all-reduce | flops 1024 | bytes 8192 | tf_op jit(solution)/shard_map/psum | solution.py:26
  23.1 7.0 all_gather.27
  31.8 3.7 fusion.46
  36.2 108.4 %reduce-scatter.10.cloned.1.call-done = f32[256,1536]{1,0:T(8,128)} async-done(((f32[1024,1536]{1,0:T(8,128)}), f32[256,1536]{1,0:T(8,128)}) %reduce-scatter.10.cloned.1.call-update) | async-done | bytes 1572880 | tf_op jit(solution)/shard_map/reduce_scatter | solution.py:67
  149.7 44.8 %all-gather.6.cloned.1.call-done = bf16[1024,2,512]{0,2,1:T(8,128)(2,1)} async-done(((bf16[256,2,512]{0,2,1:T(8,128)(2,1)}), bf16[1024,2,512]{0,2,1:T(8,128)(2,1)}) %all-gather.6.cloned.1.call-update) | async-done | bytes 2097168 | tf_op jit(solution)/shard_map/all_gather | solution.py:228
  201.1 28.5 %all-gather.8.cloned.1.call-done = bf16[1024,512]{0,1:T(8,128)(2,1)} async-done(((bf16[256,512]{0,1:T(8,128)(2,1)}), bf16[1024,512]{0,1:T(8,128)(2,1)}) %all-gather.8.cloned.1.call-update) | async-done | bytes 1048592 | tf_op jit(solution)/shard_map/all_gather | solution.py:78
  232.4 10.4 all_gather.32
  243.6 5.8 fusion.50
  253.7 10.6 all-reduce.3
  264.5 7.0 all_gather.30
  272.3 4.5 fusion.48
  276.9 121.6 %reduce-scatter.18.cloned.1.call-done = f32[256,2048]{1,0:T(8,128)} async-done(((f32[1024,2048]{1,0:T(8,128)}), f32[256,2048]{1,0:T(8,128)}) %reduce-scatter.18.cloned.1.call-update) | async-done | bytes 2097168 | tf_op jit(solution)/shard_map/reduce_scatter | solution.py:67
  398.5 147.5 %reduce-scatter.14.cloned.1.call-done = f32[256,2048]{1,0:T(8,128)} async-done(((f32[1024,2048]{1,0:T(8,128)}), f32[256,2048]{1,0:T(8,128)}) %reduce-scatter.14.cloned.1.call-update) | async-done | bytes 2097168 | tf_op jit(solution)/shard_map/reduce_scatter | solution.py:67
  546.0 3.7 fusion.7
  550.7 80.7 %all-gather.12.cloned.1.call-done = bf16[1024,2048]{1,0:T(8,128)(2,1)} async-done(((bf16[256,2048]{1,0:T(8,128)(2,1)}), bf16[1024,2048]{1,0:T(8,128)(2,1)}) %all-gather.12.cloned.1.call-update) | async-done | bytes 4194320 | tf_op jit(solution)/shard_map/all_gather | solution.py:78
  631.3 4.4 fusion.51
  635.9 77.0 %all-gather.10.cloned.1.call-done = bf16[1024,2048]{1,0:T(8,128)(2,1)} async-done(((bf16[256,2048]{1,0:T(8,128)(2,1)}), bf16[1024,2048]{1,0:T(8,128)(2,1)}) %all-gather.10.cloned.1.call-update) | async-done | bytes 4194320 | tf_op jit(solution)/shard_map/all_gather | solution.py:78
  712.9 4.7 fusion.49
  717.7 17.0 %reduce-scatter.20.cloned.1.call-done = f32[512,256]{1,0:T(8,128)} async-done(((f32[1024,256]{1,0:T(8,128)}), f32[512,256]{1,0:T(8,128)}) %reduce-scatter.20.cloned.1.call-update) | async-done | bytes 524304 | tf_op jit(solution)/shard_map/reduce_scatter | solution.py:85
  736.1 11.7 %all-reduce.2 = (f32[512]{0:T(512)S(1)}, f32[512]{0:T(512)S(1)}) all-reduce(f32[512]{0:T(512)S(1)} %get-tuple-element.124, f32[512]{0:T(512)S(1)} %get-tuple-element.128), channel_id=1, replica_groups=mesh['dp'=4,'row'=4,'col'=2] {'row'}, use_global_device_ids=true, to_apply=%region_21.22 | all-reduce | flops 1024 | bytes 8192 | tf_op jit(solution)/shard_map/psum | solution.py:26
  747.8 9.9 reduce-scatter.16.cloned.1.call-done
  760.1 8.7 all_gather.34
  770.7 44.0 %reduce-scatter.22.cloned.1.call-done = f32[256,512]{1,0:T(8,128)} async-done(((f32[1024,512]{1,0:T(8,128)}), f32[256,512]{1,0:T(8,128)}) %reduce-scatter.22.cloned.1.call-update) | async-done | bytes 524304 | tf_op jit(solution)/shard_map/reduce_scatter | solution.py:67
  815.8 3.3 fusion.8
  827.4 73.4 %reduce-scatter.24.cloned.1.call-done = f32[256,2,512]{0,2,1:T(8,128)} async-done(((f32[1024,2,512]{0,2,1:T(8,128)}), f32[256,2,512]{0,2,1:T(8,128)}) %reduce-scatter.24.cloned.1.call-update) | async-done | bytes 1048592 | tf_op jit(solution)/shard_map/reduce_scatter | solution.py:257
  904.1 64.0 %all-gather.14.cloned.1.call-done = bf16[1024,1536]{0,1:T(8,128)(2,1)} async-done(((bf16[256,1536]{0,1:T(8,128)(2,1)}), bf16[1024,1536]{0,1:T(8,128)(2,1)}) %all-gather.14.cloned.1.call-update) | async-done | bytes 3145744 | tf_op jit(solution)/shard_map/all_gather | solution.py:78
  968.1 3.9 fusion.53
  972.3 4.9 fusion.55
  987.3 11.7 %all-reduce.5 = (f32[2,512]{1,0:T(2,128)}, f32[256]{0:T(256)}, f32[2048]{0:T(1024)}, f32[256]{0:T(256)}) all-reduce(f32[2,512]{1,0:T(2,128)S(1)} %pad_maximum_fusion.3, f32[256]{0:T(256)S(1)} %convert_reduce_fusion.3, f32[2048]{0:T(1024)S(1)} %convert_reduce_fusion, ...), channel_id=1, replica_groups=mesh['dp'=4,'row'=4,'col'=2] {'dp'}, use_global_device_ids=true, to_apply=%region_36.37 | all-reduce | flops 3584 | bytes 28672 | tf_op jit(solution)/shard_map/psum | solution.py:297
  1000.6 14.2 %all-reduce = (f32[256]{0:T(256)}, f32[256]{0:T(256)}, f32[256]{0:T(256)}, f32[256]{0:T(256)}) all-reduce(f32[256]{0:T(256)S(1)} %get-tuple-element.125, f32[256]{0:T(256)S(1)} %get-tuple-element.130, f32[256]{0:T(256)S(1)} %get-tuple-element.123, f32[256]{0:T(256)S(1)} %get-tuple-element.129), channel_id=1, replica_groups=mesh['dp'=4,'row'=4,'col'=2] {'dp','col'}, use_global_device_ids=true, to_apply=%region_31.32 | all-reduce | flops 1024 | bytes 8192 | tf_op jit(solution)/shard_map/psum | solution.py:316
  1014.8 8.9 all-reduce.1
  1025.9 88.7 %all-reduce.9.cloned.1.call-done = (f32[256,3,512]{0,2,1:T(8,128)}, f32[512,256]{1,0:T(8,128)}, f32[256,2048]{1,0:T(8,128)}, f32[2048,256]{1,0:T(8,128)}) async-done(((f32[256,3,512]{0,2,1:T(8,128)}, f32[512,256]{1,0:T(8,128)}, f32[256,2048]{1,0:T(8,128)}, f32[2048,256]{1,0:T(8,128)}), (f32[256,3,512]{0,2,1:T(8,128)}, f32[512,256]{1,0:T(8,128)}, f32[256,2048]{1,0:T(8,128)}, ...) | async-done | bytes 6291472 | tf_op jit(solution)/shard_map/psum | solution.py:297
  (163 shorter events, 65.3 us)
Async XLA Ops:
  7.2 265.1 %copy-start = (bf16[256,2048]{1,0:T(8,128)(2,1)S(1)}, bf16[256,2048]{1,0:T(8,128)(2,1)}, u32[]{:S(2)}) copy-start(bf16[256,2048]{1,0:T(8,128)(2,1)} %param.28) | copy-start | bytes 3145732
  7.2 137.4 %reduce-scatter.10.cloned.1.call-start = ((), (), s32[]{:S(2)}) async-start(), calls=%async_computation.9 | async-start | bytes 7864320 | tf_op jit(solution)/shard_map/reduce_scatter | solution.py:67
  30.2 5.3 copy-start.9
  35.5 159.0 %all-gather.6.cloned.1.call-start = ((), (), s32[]{:S(2)}) async-start(), calls=%async_computation.10 | async-start | bytes 2621440 | tf_op jit(solution)/shard_map/all_gather | solution.py:228
  36.2 111.5 %copy-start.26 = (s32[1024]{0:T(1024)S(1)}, s32[1024]{0:T(1024)}, u32[]{:S(2)}) copy-start(s32[1024]{0:T(1024)} %param.19) | copy-start | bytes 12292
  36.2 111.7 %copy-start.35 = (s32[13]{0:T(128)S(1)}, s32[13]{0:T(128)}, u32[]{:S(2)}) copy-start(s32[13]{0:T(128)} %param.18) | copy-start | bytes 160
  146.7 49.7 %copy-start.19 = (f32[256,1,512]{0,2,1:T(8,128)}, f32[256,1,512]{0,2,1:T(8,128)S(1)}, u32[]{:S(2)}) copy-start(f32[256,1,512]{0,2,1:T(8,128)S(1)} %get-tuple-element.162) | copy-start | bytes 1572868
  147.6 82.1 %all-gather.8.cloned.1.call-start = ((), (), s32[]{:S(2)}) async-start(), calls=%async_computation.11 | async-start | bytes 1310720 | tf_op jit(solution)/shard_map/all_gather | solution.py:78
  199.2 30.5 %copy-start.24 = (bf16[512,256]{1,0:T(8,128)(2,1)S(1)}, bf16[512,256]{1,0:T(8,128)(2,1)}, u32[]{:S(2)}) copy-start(bf16[512,256]{1,0:T(8,128)(2,1)} %param.24) | copy-start | bytes 786436
  201.1 31.4 %copy-start.23 = (bf16[512,256]{1,0:T(8,128)(2,1)S(1)}, bf16[512,256]{1,0:T(8,128)(2,1)}, u32[]{:S(2)}) copy-start(bf16[512,256]{1,0:T(8,128)(2,1)} %param.17) | copy-start | bytes 786436
  201.1 51.3 %reduce-scatter.12.cloned.1.call-start = ((), (), s32[]{:S(2)}) async-start(), calls=%async_computation.12 | async-start | bytes 1572864 | tf_op jit(solution)/shard_map/reduce_scatter | solution.py:85
  232.4 166.1 %reduce-scatter.18.cloned.1.call-start = ((), (), s32[]{:S(2)}) async-start(), calls=%async_computation.16 | async-start | bytes 10485760 | tf_op jit(solution)/shard_map/reduce_scatter | solution.py:67
  249.4 14.9 %copy-start.27 = (f32[256]{0:T(256)S(1)}, f32[256]{0:T(256)}, u32[]{:S(2)}) copy-start(f32[256]{0:T(256)} %param.26) | copy-start | bytes 3076
  249.4 14.9 %copy-start.31 = (f32[256]{0:T(256)S(1)}, f32[256]{0:T(256)}, u32[]{:S(2)}) copy-start(f32[256]{0:T(256)} %param.27) | copy-start | bytes 3076
  249.4 296.6 %reduce-scatter.14.cloned.1.call-start = ((), (), s32[]{:S(2)}) async-start(), calls=%async_computation.13 | async-start | bytes 10485760 | tf_op jit(solution)/shard_map/reduce_scatter | solution.py:67
  276.8 269.2 %copy-start.29 = (f32[2048]{0:T(1024)S(1)}, f32[2048]{0:T(1024)}, u32[]{:S(2)}) copy-start(f32[2048]{0:T(1024)} %param.29) | copy-start | bytes 24580
  276.8 354.5 %all-gather.12.cloned.1.call-start = ((), (), s32[]{:S(2)}) async-start(), calls=%async_computation.17 | async-start | bytes 5242880 | tf_op jit(solution)/shard_map/all_gather | solution.py:78
  549.7 163.2 %all-gather.10.cloned.1.call-start = ((), (), s32[]{:S(2)}) async-start(), calls=%async_computation.14 | async-start | bytes 5242880 | tf_op jit(solution)/shard_map/all_gather | solution.py:78
  550.5 184.2 %reduce-scatter.20.cloned.1.call-start = ((), (), s32[]{:S(2)}) async-start(), calls=%async_computation.18 | async-start | bytes 1572864 | tf_op jit(solution)/shard_map/reduce_scatter | solution.py:85
  635.8 121.9 %copy-start.32 = (f32[256]{0:T(256)S(1)}, f32[256]{0:T(256)}, u32[]{:S(2)}) copy-start(f32[256]{0:T(256)} %param.31) | copy-start | bytes 3076
  635.8 121.9 %reduce-scatter.16.cloned.1.call-start = ((), (), s32[]{:S(2)}) async-start(), calls=%async_computation.15 | async-start | bytes 1572864 | tf_op jit(solution)/shard_map/reduce_scatter | solution.py:85
  717.6 97.0 %reduce-scatter.22.cloned.1.call-start = ((), (), s32[]{:S(2)}) async-start(), calls=%async_computation.19 | async-start | bytes 2621440 | tf_op jit(solution)/shard_map/reduce_scatter | solution.py:67
  770.6 130.2 %reduce-scatter.24.cloned.1.call-start = ((), (), s32[]{:S(2)}) async-start(), calls=%async_computation.20 | async-start | bytes 5242880 | tf_op jit(solution)/shard_map/reduce_scatter | solution.py:257
  824.6 143.5 %all-gather.14.cloned.1.call-start = ((), (), s32[]{:S(2)}) async-start(), calls=%async_computation.21 | async-start | bytes 3932160 | tf_op jit(solution)/shard_map/all_gather | solution.py:78
  827.4 140.7 %copy-start.14 = (bf16[256,3,512]{0,2,1:T(8,128)(2,1)S(1)}, bf16[256,3,512]{0,2,1:T(8,128)(2,1)}, u32[]{:S(2)}) copy-start(bf16[256,3,512]{0,2,1:T(8,128)(2,1)} %copy-done.13) | copy-start | bytes 2359300
  904.0 68.3 %copy-start.16 = (bf16[1024,256]{1,0:T(8,128)(2,1)S(1)}, bf16[1024,256]{1,0:T(8,128)(2,1)}, u32[]{:S(2)}) copy-start(bf16[1024,256]{1,0:T(8,128)(2,1)} %copy-done.15) | copy-start | bytes 1572868
  904.0 95.0 %reduce-scatter.26.cloned.1.call-start = ((), (), s32[]{:S(2)}) async-start(), calls=%async_computation.22 | async-start | bytes 1572864 | tf_op jit(solution)/shard_map/reduce_scatter | solution.py:85
  972.0 5.2 copy-start.6
  972.0 142.6 %all-reduce.9.cloned.1.call-start = ((), (), s32[]{:S(2)}) async-start(), calls=%async_computation.23 | async-start | bytes 12582912 | tf_op jit(solution)/shard_map/psum | solution.py:297
  972.3 4.9 copy-start.34
  983.6 15.4 %copy-start.28 = (f32[256]{0:T(256)S(1)}, f32[256]{0:T(256)}, u32[]{:S(2)}) copy-start(f32[256]{0:T(256)} %param.20) | copy-start | bytes 3076
  986.6 37.1 %copy-start.21 = (f32[512,256]{1,0:T(8,128)S(1)}, f32[512,256]{1,0:T(8,128)}, u32[]{:S(2)}) copy-start(f32[512,256]{1,0:T(8,128)} %get-tuple-element.156) | copy-start | bytes 1572868
  (19 other events, 49.0 us)
Sparse Core Ops, SparseCore 0:
  35.6 108.9 reduce-scatter.9
  147.7 46.7 all-gather.5
  201.2 28.4 all-gather.7
  232.5 19.8 reduce-scatter.11
  254.7 143.6 reduce-scatter.17
  400.8 145.1 reduce-scatter.13
  549.8 81.4 all-gather.11
  633.6 79.2 all-gather.9
  715.8 18.8 reduce-scatter.19
  737.3 20.3 reduce-scatter.15
  770.7 43.8 reduce-scatter.21
  824.7 76.0 reduce-scatter.23
  904.1 63.9 all-gather.13
  972.2 18.4 reduce-scatter.25
  994.3 120.2 all-reduce.8
where the time goes:
time: 1130 us
  waiting for transfers between devices  909 us (80%)
  blocking collectives  104 us (9%)
  matrix products  53.8 us (5%)
  other arithmetic  30.3 us (3%)
  local copies, waits for them, and re-layouts  15.1 us (1%)
  between operations  14.3 us (1%)
    reduce_scatter x4, waiting for transfers between devices, across_rows(): lax.psum_scatter(partial_term(jnp.int32(0), row_count * lax.axis_size('ro...  422 us
    all_gather x4, waiting for transfers between devices, across_cols(): gathered = lax.all_gather(operand, 'row', axis=0, tiled=True)  250 us
    psum x1, waiting for transfers between devices, on_device(): lax.psum((weight_terms[0], weight_terms[1], weight_terms[2], weight_terms...  88.7 us
    reduce_scatter x1, waiting for transfers between devices, on_device(): lax.psum_scatter(jnp.stack([key_grad.reshape(-1, col_width), value_grad.r...  73.4 us
    all_gather x1, waiting for transfers between devices, on_device(): lax.all_gather(jnp.stack([keys_here, values_here], axis=1), 'row', axis=0...  44.8 us
    psum x4, blocking collectives, width_sums(): lax.psum((jnp.sum(first_term, axis=1), jnp.sum(second_term, axis=1)), 'row')  44.6 us
    all_gather x4, blocking collectives, across_rows(): gathered = lax.all_gather(operand, 'col', axis=0, tiled=True)  33.2 us
    reduce_scatter x4, waiting for transfers between devices, across_cols(): lax.psum_scatter(partial_term(jnp.int32(0), row_count * lax.axis_size('co...  29.8 us
  transfers between devices with their start and end apart: 15, of which 14 were waited for; matrix products, arithmetic and copies ran while one was open for 4% of the time, Pallas kernels for 0%

commit v1 on v0

--- a/solution.py
+++ b/solution.py
@@ -1,9 +1,17 @@
+import functools
 import math
 
 import jax
 import jax.numpy as jnp
 from jax import lax
+from jax.experimental import pallas as pl
+from jax.experimental.pallas import tpu as pltpu
 from jax.sharding import PartitionSpec as P
+
+MESH = pl.DeviceIdType.MESH
+BF = jnp.bfloat16
+F32 = jnp.float32
+
 
 HD = 128
 
@@ -334,6 +342,779 @@
     )
 
 
+RELS = (0, 4, 2, 6)
+
+
+def dot_nn(a, b):
+    return lax.dot_general(a, b, (((1,), (0,)), ((), ())), preferred_element_type=F32)
+
+
+def dot_nt(a, b):
+    return lax.dot_general(a, b, (((1,), (1,)), ((), ())), preferred_element_type=F32)
+
+
+def dot_tn(a, b):
+    return lax.dot_general(a, b, (((0,), (0,)), ((), ())), preferred_element_type=F32)
+
+
+def span(index, size):
+    return pl.ds(pl.multiple_of(index * size, size), size)
+
+
+class Net:
+    def __init__(self, ssem, rsem):
+        self.dp = lax.axis_index("dp")
+        self.row = lax.axis_index("row")
+        self.col = lax.axis_index("col")
+        self.y, self.k = self.dp // 2, self.dp % 2
+        self.zh, self.zl = self.row // 2, self.row % 2
+        self.x = self.col
+        self.slot = self.x * 4 + self.zl * 2 + self.k
+        self.chip = self.x * 2 + self.zl
+        self.slice = self.zl * 2 + self.k
+        self.ssem, self.rsem = ssem, rsem
+        self.used = 0
+        self.pending = []
+
+    def sites(self, n):
+        first = self.used
+        self.used += n
+        return first
+
+    def peer(self, dy=0, dk=0, dz=0, dx=0):
+        return (
+            (self.y ^ dy) * 2 + (self.k ^ dk),
+            self.row ^ dz,
+            self.col ^ dx,
+        )
+
+    def rel(self, rel):
+        return self.peer(dz=(rel >> 1) & 1, dx=rel >> 2, dk=rel & 1)
+
+    def make(self, src, dst, site, device, recv_site=None):
+        recv = site if recv_site is None else recv_site
+        return pltpu.make_async_remote_copy(
+            src_ref=src,
+            dst_ref=dst,
+            send_sem=self.ssem.at[site],
+            recv_sem=self.rsem.at[recv],
+            device_id=device,
+            device_id_type=MESH,
+        )
+
+    def send(self, src, dst, site, device, recv_site=None, skip=None):
+        remote = self.make(src, dst, site, device, recv_site)
+        if skip is None:
+            remote.start()
+        else:
+            recv = site if recv_site is None else recv_site
+
+            @pl.when(skip)
+            def _():
+                pltpu.make_async_copy(src, dst, self.rsem.at[recv]).start()
+
+            @pl.when(jnp.logical_not(skip))
+            def _():
+                remote.start()
+
+        self.pending.append((remote, skip))
+        return remote
+
+    def landed(self, ref, site):
+        self.make(ref, ref, site, self.peer(dk=1)).wait_recv()
+
+    def drain(self, upto=None):
+        for remote, skip in self.pending:
+            if skip is None:
+                remote.wait_send()
+            else:
+
+                @pl.when(jnp.logical_not(skip))
+                def _(remote=remote):
+                    remote.wait_send()
+
+        self.pending = []
+
+
+class Gather:
+    def __init__(self, net, buf):
+        self.net, self.buf = net, buf
+        self.first = net.sites(7)
+
+    def start(self):
+        net, buf = self.net, self.buf
+        own = buf.at[net.slot]
+        net.send(own, own, self.first, net.rel(1))
+        for j in (1, 2, 3):
+            net.send(own, own, self.first + j, net.rel(RELS[j]))
+
+    def relay(self, j):
+        net, buf = self.net, self.buf
+        part = buf.at[net.slot ^ RELS[j]]
+        net.landed(part, self.first + j)
+        net.send(part, part, self.first + 3 + j, net.rel(1))
+
+    def ready(self, j):
+        net, buf = self.net, self.buf
+        part = buf.at[net.slot ^ RELS[j] ^ 1]
+        net.landed(part, self.first if j == 0 else self.first + 3 + j)
+
+    def block(self, j):
+        chip = self.net.chip ^ (RELS[j] >> 1)
+        both = self.buf[pl.ds(chip * 2, 2)]
+        return both.reshape(2 * both.shape[1], both.shape[2])
+
+
+class Scatter:
+    def __init__(self, net, part, hop, land_one, land_two):
+        self.net, self.part, self.hop_buf = net, part, hop
+        self.one, self.two = land_one, land_two
+        self.first = net.sites(7)
+        self.sent = []
+
+    def put(self, j, value):
+        net = self.net
+        chip = net.chip ^ (RELS[j] >> 1)
+        shard = self.part.shape[1]
+        self.part[pl.ds(chip * 2, 2)] = value.astype(BF).reshape(2, shard, value.shape[1])
+        self.push(j)
+
+    def push(self, j):
+        net = self.net
+        chip = net.chip ^ (RELS[j] >> 1)
+        self.sent.append(
+            net.send(
+                self.part.at[chip * 2 + (1 - net.k)],
+                self.one.at[j],
+                self.first + j,
+                net.rel(1),
+            )
+        )
+
+    def chip_sum(self, j):
+        net = self.net
+        chip = net.chip ^ (RELS[j] >> 1)
+        net.landed(self.one.at[j], self.first + j)
+        return self.part[chip * 2 + net.k].astype(F32) + self.one[j].astype(F32)
+
+    def hop(self, j):
+        net = self.net
+        self.hop_buf[j - 1] = self.chip_sum(j).astype(BF)
+        self.sent.append(
+            net.send(
+                self.hop_buf.at[j - 1],
+                self.two.at[j - 1],
+                self.first + 3 + j,
+                net.rel(RELS[j]),
+            )
+        )
+
+    def left(self):
+        for remote in self.sent:
+            remote.wait_send()
+        mine = {id(remote) for remote in self.sent}
+        self.net.pending = [p for p in self.net.pending if id(p[0]) not in mine]
+
+    def total(self):
+        net = self.net
+        value = self.chip_sum(0)
+        for j in (1, 2, 3):
+            net.landed(self.two.at[j - 1], self.first + 3 + j)
+            value = value + self.two[j - 1].astype(F32)
+        return value
+
+
+class TreeSum:
+    def __init__(self, net, own, land_y, hop, land_z, done, out):
+        self.net, self.own, self.land_y = net, own, land_y
+        self.hop_buf, self.land_z, self.done, self.out = hop, land_z, done, out
+        self.first = net.sites(8)
+
+    def start(self):
+        net = self.net
+        net.send(self.own.at[:, 1 - net.y], self.land_y, self.first, net.peer(dy=1))
+
+    def across(self):
+        net = self.net
+        net.landed(self.land_y, self.first)
+        far = 1 - net.zh
+        self.hop_buf[...] = (
+            self.own[far, net.y].astype(F32) + self.land_y[far].astype(F32)
+        ).astype(BF)
+        net.send(self.hop_buf, self.land_z, self.first + 1, net.peer(dz=2))
+
+    def hand_out(self):
+        net = self.net
+        net.landed(self.land_z, self.first + 1)
+        self.done[...] = (
+            self.own[net.zh, net.y].astype(F32)
+            + self.land_y[net.zh].astype(F32)
+            + self.land_z[...].astype(F32)
+        ).astype(BF)
+        place = self.out.at[net.slice]
+        target = net.zh * 2 + net.y
+        for step in (0, 1):
+            net.send(
+                self.done,
+                place,
+                self.first + 2 + step,
+                ((net.y ^ step) * 2 + net.k, target, net.col),
+                recv_site=self.first + 4 + net.zl,
+                skip=(target == net.row) if step == 0 else None,
+            )
+
+    def share(self):
+        net = self.net
+        for low in (0, 1):
+            part = self.out.at[low * 2 + net.k]
+            net.landed(part, self.first + 4 + low)
+            net.send(part, part, self.first + 6 + low, net.rel(1))
+
+    def finish(self):
+        net = self.net
+        for low in (0, 1):
+            net.landed(self.out.at[low * 2 + (1 - net.k)], self.first + 6 + low)
+
+
+def layer_kernel(eps, masked, sems, *refs):
+    (
+        inp, cot, w_q, w_o, w_d, w_u, tab, vec_in, b_up, b_qv,
+        res_out, grad_out, out_q, out_o, out_d, out_u, out_tok, out_small,
+        xs, e1, g, e2, gb, wq, wo, wd, wu, tab_far, vec, bias,
+        q_buf, k_buf, v_buf, p_buf, mix, mix_b,
+        part_a, part_b, hop_a, hop_b, one, two,
+        gh, hid, gp, gm, dk_acc, dv_acc, dqkv, mid, gmid, back_a, back_b,
+        dw_q, dw_o, dw_d, dw_u, ly_q, ly_o, ly_d, ly_u,
+        yh_q, yh_o, yh_d, yh_u, lz_q, lz_o, lz_d, lz_u,
+        fin_q, fin_o, fin_d, fin_u,
+        tok, tok_one, tok_sum, tok_two, small, small_land, small_sum,
+        ssem, rsem, lsem,
+    ) = refs
+    net = Net(ssem, rsem)
+    y, k, zh, zl, x, row = net.y, net.k, net.zh, net.zl, net.x, net.row
+    shard, width = xs.shape
+    tokens = 8 * shard
+    quarter = width // 4
+    head = q_buf.shape[1]
+
+    greet = [
+        net.peer(dy=dy, dk=dk, dz=dz)
+        for dy in (0, 1)
+        for dk in (0, 1)
+        for dz in (0, 1, 2, 3)
+        if dy + dk + dz
+    ]
+    greet += [net.peer(dk=dk, dz=dz, dx=1) for dk in (0, 1) for dz in (0, 1)]
+    barrier = pltpu.get_barrier_semaphore()
+    for device in greet:
+        pl.semaphore_signal(barrier, inc=1, device_id=device, device_id_type=MESH)
+    pl.semaphore_wait(barrier, len(greet))
+
+    def send_home(src, dst_of, first):
+        for s in range(4):
+            low, core = s // 2, s % 2
+            target = 2 * k + low
+            net.send(
+                src.at[span(s, shard), :],
+                dst_of(s).at[:, span(row, quarter)],
+                first + s,
+                (y * 2 + core, target, net.col),
+                recv_site=first + 4 + row,
+                skip=(target == row) & (k == core),
+            )
+
+    def home_ready(dst, first):
+        for z in range(4):
+            net.landed(dst.at[:, span(z, quarter)], first + 4 + z)
+
+    home_x, home_g = net.sites(8), net.sites(8)
+    send_home(inp, lambda s: xs, home_x)
+
+    vec_site = net.sites(3)
+    for o in (1, 2, 3):
+        net.send(
+            vec_in, vec.at[:, span(row, quarter)], vec_site + o - 1, net.peer(dz=o)
+        )
+    tab_site = net.sites(1)
+    net.send(tab, tab_far, tab_site, net.rel(1))
+
+    def slices(w_ref, full, axis):
+        if axis == 0:
+            rows = full.shape[0] // 4
+            return rows, lambda z: full.at[span(z, rows), :]
+        cols = full.shape[1] // 4
+        return full.shape[0], lambda z: full.at[:, span(z, cols)]
+
+    class Weight:
+        def __init__(self, src_of, full, axis, local):
+            self.src_of, self.full = src_of, full
+            self.rows, self.place = slices(None, full, axis)
+            self.first = net.sites(6)
+            self.local = local
+
+        def half(self, ref, which):
+            rows = self.rows // 2
+            return ref.at[span(which, rows), :]
+
+        def start(self):
+            own = pltpu.make_async_copy(
+                self.src_of(net.slice), self.place(row), lsem.at[self.local]
+            )
+            own.start()
+            for o in (1, 2, 3):
+                far = (zl ^ (o & 1)) * 2 + k
+                net.send(
+                    self.half(self.src_of(far), y),
+                    self.half(self.place(row), y),
+                    self.first + o - 1,
+                    net.peer(dz=o),
+                )
+            self.own = own
+
+        def relay(self):
+            for o in (1, 2, 3):
+                part = self.half(self.place(row ^ o), y)
+                net.landed(part, self.first + o - 1)
+                net.send(part, part, self.first + 2 + o, net.peer(dy=1))
+
+        def ready(self):
+            for o in (1, 2, 3):
+                net.landed(self.half(self.place(row ^ o), 1 - y), self.first + 2 + o)
+            self.own.wait()
+
+    hidden = hid.shape[1]
+    weight_q = Weight(lambda s: w_q.at[s], wq, 0, 0)
+    weight_o = Weight(lambda s: w_o.at[span(s, head), :], wo, 1, 1)
+    weight_d = Weight(lambda s: w_d.at[span(s, hidden), :], wd, 1, 2)
+    weight_u = Weight(lambda s: w_u.at[:, span(s, hidden)], wu, 0, 3)
+    weight_q.start()
+    send_home(cot, lambda s: g.at[x * 4 + s], home_g)
+    weight_o.start()
+
+    vec[:, span(row, quarter)] = vec_in[...]
+    for o in (1, 2, 3):
+        net.landed(vec.at[:, span(row ^ o, quarter)], vec_site + o - 1)
+
+    def norm_stats(values):
+        mean = jnp.sum(values, axis=1, keepdims=True) * (1.0 / width)
+        msq = jnp.sum(values * values, axis=1, keepdims=True) * (1.0 / width)
+        inv = lax.rsqrt(msq - mean * mean + eps)
+        return (values - mean) * inv, inv
+
+    home_ready(xs, home_x)
+    normed, _ = norm_stats(xs[...].astype(F32))
+    e1[net.slot] = (normed * vec[0:1, :] + vec[1:2, :]).astype(BF)
+    gather_e1 = Gather(net, e1)
+    gather_e1.start()
+    gather_g = Gather(net, g)
+    weight_d.start()
+    weight_u.start()
+    weight_q.relay()
+    home_ready(g.at[net.slot], home_g)
+
+    net.landed(tab_far, tab_site)
+    table = jnp.where(zh == k, tab[...], tab_far[...])
+    exponent = jnp.full((1, tokens), -(x * 4 + net.slice + 1), jnp.int32).astype(F32)
+    slope = jnp.exp2(exponent)
+    bias[...] = jnp.where(table >= 0.0, slope * table, masked)
+
+    b_q = b_qv[0:1, span(net.slice, head)]
+    b_v = b_qv[1:2, span(net.slice, head)]
+    weight_q.ready()
+    for j in range(4):
+        if j:
+            gather_e1.relay(j)
+        if j == 3:
+            gather_g.start()
+        gather_e1.ready(j)
+        rows = span(net.chip ^ (RELS[j] >> 1), 2 * shard)
+        proj = dot_nn(gather_e1.block(j), wq[...])
+        q_buf[rows, :] = (proj[:, :head] + b_q).astype(BF)
+        k_buf[rows, :] = proj[:, head : 2 * head].astype(BF)
+        v_buf[rows, :] = (proj[:, 2 * head :] + b_v).astype(BF)
+    weight_o.relay()
+
+    scale = head ** (-0.5)
+    seg_len = tokens // 16
+    key_at = lax.broadcasted_iota(jnp.int32, (1, tokens), 1)
+    key_half = key_at // seg_len
+    key_seg = jnp.maximum(key_half - 3, 0)
+
+    def attend(i, carry):
+        first = pl.multiple_of(i * shard, shard)
+        raw = dot_nt(q_buf[pl.ds(first, shard), :], k_buf[...])
+        parts = []
+        for half in (0, 1):
+            at = 2 * i + half
+            seg = jnp.maximum(at - 3, 0)
+            later = jnp.where(key_seg == seg, key_at, -1)
+            query_at = first + half * seg_len + lax.broadcasted_iota(jnp.int32, (seg_len, 1), 0)
+            scores = raw[half * seg_len : (half + 1) * seg_len] * scale + bias[pl.ds(at, 1), :]
+            scores = jnp.where(later > query_at, masked, scores)
+            top = jnp.max(scores, axis=1, keepdims=True)
+            weights = jnp.exp(scores - top)
+            norm = 1.0 / jnp.sum(weights, axis=1, keepdims=True)
+            parts.append((weights * norm).astype(BF))
+        probs = jnp.concatenate(parts, axis=0)
+        p_buf[pl.ds(first, shard), :] = probs
+        mixed = dot_nn(probs, v_buf[...])
+        mix[pl.ds(first, shard), :] = mixed
+        mix_b[pl.ds(first, shard), :] = mixed.astype(BF)
+        return carry
+
+    lax.fori_loop(0, 8, attend, 0)
+
+    for j in (1, 2, 3):
+        gather_g.relay(j)
+    weight_o.ready()
+
+    def rows_of(j):
+        return span(net.chip ^ (RELS[j] >> 1), 2 * shard)
+
+    order = (3, 1, 2, 0)
+    scatter = Scatter(net, part_a, hop_a, one.at[0], two.at[0])
+    for j in order:
+        scatter.put(j, dot_nn(mix_b[rows_of(j), :], wo[...]))
+    for j in (3, 1, 2):
+        scatter.hop(j)
+    weight_d.relay()
+    weight_u.relay()
+    weight_d.ready()
+    gather_g.ready(0)
+    gather_g.ready(1)
+    gather_g.ready(2)
+    gather_g.ready(3)
+
+    def hidden_grad(c, carry):
+        rows = span(c, 2 * shard)
+        both = g[pl.ds(c * 2, 2)].reshape(2 * shard, width)
+        gh[rows, :] = dot_nt(both, wd[...])
+        return carry
+
+    lax.fori_loop(0, 4, hidden_grad, 0)
+
+    middle = xs[...].astype(F32) + scatter.total() + vec[2:3, :]
+    mid[...] = middle
+    normed, _ = norm_stats(middle)
+    e2[net.slot] = (normed * vec[3:4, :] + vec[4:5, :]).astype(BF)
+    gather_e2 = Gather(net, e2)
+    gather_e2.start()
+    scatter.left()
+
+    b_u = b_up[0:1, span(net.slice, hidden)]
+    weight_u.ready()
+    scatter_two = Scatter(net, part_a, hop_a, one.at[1], two.at[1])
+    for j in range(4):
+        if j:
+            gather_e2.relay(j)
+        gather_e2.ready(j)
+        pre = dot_nn(gather_e2.block(j), wu[...]) + b_u
+        bell = 0.5 * (1.0 + lax.erf(pre * (1.0 / math.sqrt(2.0))))
+        hid[rows_of(j), :] = (pre * bell).astype(BF)
+        rise = bell + pre * jnp.exp(-0.5 * pre * pre) * (1.0 / math.sqrt(2.0 * math.pi))
+        gp[rows_of(j), :] = (gh[rows_of(j), :] * rise).astype(BF)
+        scatter_two.put(j, dot_nt(gp[rows_of(j), :], wu[...]))
+        if j > 1:
+            scatter_two.hop(j - 1)
+    scatter_two.hop(3)
+
+    sum_d = TreeSum(net, dw_d, ly_d, yh_d, lz_d, fin_d, out_d)
+    sum_u = TreeSum(net, dw_u, ly_u, yh_u, lz_u, fin_u, out_u)
+    sum_o = TreeSum(net, dw_o, ly_o, yh_o, lz_o, fin_o, out_o)
+    sum_q = TreeSum(net, dw_q, ly_q, yh_q, lz_q, fin_q, out_q)
+
+    def columns(buf, z):
+        part = buf[:, :, span(z, quarter)]
+        return part.reshape(tokens, quarter)
+
+    def grad_down(z, carry):
+        dw_d[z // 2, z % 2] = dot_tn(hid[...], columns(g, z)).astype(BF)
+        return carry
+
+    lax.fori_loop(0, 4, grad_down, 0)
+    sum_d.start()
+
+    grad = scatter_two.total()
+    middle = mid[...]
+    normed, inv = norm_stats(middle)
+    tok[2:3, :] = jnp.sum(grad * normed, axis=0, keepdims=True)
+    tok[3:4, :] = jnp.sum(grad, axis=0, keepdims=True)
+    spread = grad * vec[3:4, :]
+    mean_one = jnp.sum(spread, axis=1, keepdims=True) * (1.0 / width)
+    mean_two = jnp.sum(spread * normed, axis=1, keepdims=True) * (1.0 / width)
+    cot_own = g[net.slot].astype(F32)
+    tok[5:6, :] = jnp.sum(cot_own, axis=0, keepdims=True)
+    total = cot_own + inv * (spread - mean_one - normed * mean_two)
+    gmid[...] = total
+    branch = total.astype(BF)
+    gb[net.slot] = branch
+    tok[4:5, :] = jnp.sum(branch.astype(F32), axis=0, keepdims=True)
+    tok[6:8, :] = jnp.zeros((2, width), F32)
+    gather_gb = Gather(net, gb)
+    gather_gb.start()
+
+    scatter_three = Scatter(net, part_b, hop_b, one.at[2], two.at[2])
+    for j in order:
+        scatter_three.put(j, dot_nn(hid[rows_of(j), :], wd[...]))
+
+    dk_acc[...] = jnp.zeros_like(dk_acc)
+    dv_acc[...] = jnp.zeros_like(dv_acc)
+
+    def attend_back(first):
+        rows = pl.ds(first, shard)
+        grad_mix = gm[rows, :]
+        probs = p_buf[rows, :]
+        grad_probs = dot_nt(grad_mix, v_buf[...])
+        centre = jnp.sum(mix[rows, :] * grad_mix.astype(F32), axis=1, keepdims=True)
+        grad_scores = (probs.astype(F32) * (grad_probs - centre)).astype(BF)
+        dqkv[rows, :head] = (dot_nn(grad_scores, k_buf[...]) * scale).astype(BF)
+        dk_acc[...] += dot_tn(grad_scores, q_buf[rows, :])
+        dv_acc[...] += dot_tn(probs, grad_mix)
+
+    for j in range(4):
+        if j:
+            gather_gb.relay(j)
+        gather_gb.ready(j)
+        chip = net.chip ^ (RELS[j] >> 1)
+        gm[rows_of(j), :] = dot_nt(gather_gb.block(j), wo[...]).astype(BF)
+
+        def two_tiles(t, carry, chip=chip):
+            attend_back(pl.multiple_of((chip * 2 + t) * shard, shard))
+            return carry
+
+        lax.fori_loop(0, 2, two_tiles, 0)
+    dqkv[:, head : 2 * head] = (dk_acc[...] * scale).astype(BF)
+    dqkv[:, 2 * head :] = dv_acc[...].astype(BF)
+
+    for j in (3, 1, 2):
+        scatter_three.hop(j)
+    scatter_two.left()
+    scatter_four = Scatter(net, part_a, hop_a, one.at[3], two.at[3])
+    for j in order:
+        scatter_four.put(j, dot_nt(dqkv[rows_of(j), :], wq[...]))
+    for j in (3, 1, 2):
+        scatter_four.hop(j)
+
+    def grad_qkv(z, carry):
+        dw_q[z // 2, z % 2] = dot_tn(columns(e1, z), dqkv[...]).astype(BF)
+        return carry
+
+    lax.fori_loop(0, 4, grad_qkv, 0)
+    sum_q.start()
+
+    def grad_up(z, carry):
+        dw_u[z // 2, z % 2] = dot_tn(columns(e2, z), gp[...]).astype(BF)
+        return carry
+
+    lax.fori_loop(0, 4, grad_up, 0)
+    sum_u.start()
+
+    def grad_o(z, carry):
+        dw_o[z // 2, z % 2] = dot_tn(mix_b[...], columns(gb, z)).astype(BF)
+        return carry
+
+    lax.fori_loop(0, 4, grad_o, 0)
+    sum_o.start()
+
+    small[...] = jnp.zeros_like(small)
+    small[0:1, :] = jnp.sum(gp[...].astype(F32), axis=0, keepdims=True)
+    small[1:2, :head] = jnp.sum(dqkv[:, :head].astype(F32), axis=0, keepdims=True)
+    small[1:2, head : 2 * head] = jnp.sum(dqkv[:, 2 * head :].astype(F32), axis=0, keepdims=True)
+    small_site = net.sites(6)
+    others = ((1, 0), (0, 2), (1, 2))
+    for n, (dy, dz) in enumerate(others):
+        net.send(small, small_land.at[n], small_site + n, net.peer(dy=dy, dz=dz))
+
+    def send_out(src, dst, first):
+        for z in range(4):
+            net.send(
+                src.at[:, span(z, quarter)],
+                dst.at[span(net.slice, shard), :],
+                first + z,
+                (y * 2 + zh, z, net.col),
+                recv_site=first + 4 + net.slice,
+                skip=(row == z) & (k == zh),
+            )
+
+    def out_ready(dst, first):
+        for s in range(4):
+            net.landed(dst.at[span(s, shard), :], first + 4 + s)
+
+    res_site, grad_site = net.sites(8), net.sites(8)
+    back_a[...] = (mid[...] + scatter_three.total() + vec[5:6, :]).astype(BF)
+    send_out(back_a, res_out, res_site)
+
+    grad = scatter_four.total()
+    normed, inv = norm_stats(xs[...].astype(F32))
+    tok[0:1, :] = jnp.sum(grad * normed, axis=0, keepdims=True)
+    tok[1:2, :] = jnp.sum(grad, axis=0, keepdims=True)
+    tok_site = net.sites(10)
+    for n in range(1, 8):
+        net.send(tok, tok_one.at[n - 1], tok_site + n - 1, net.rel(n))
+    spread = grad * vec[0:1, :]
+    mean_one = jnp.sum(spread, axis=1, keepdims=True) * (1.0 / width)
+    mean_two = jnp.sum(spread * normed, axis=1, keepdims=True) * (1.0 / width)
+    back_b[...] = (gmid[...] + inv * (spread - mean_one - normed * mean_two)).astype(BF)
+    send_out(back_b, grad_out, grad_site)
+
+    sums = (sum_d, sum_q, sum_u, sum_o)
+    for one_sum in sums:
+        one_sum.across()
+    acc = small[...]
+    for n in range(3):
+        net.landed(small_land.at[n], small_site + n)
+        acc = acc + small_land[n]
+    small_sum[...] = acc
+    out_small[net.slice] = acc
+    for n, (dk, dz) in enumerate(((1, 0), (0, 1), (1, 1))):
+        net.send(
+            small_sum, out_small.at[net.slice], small_site + 3 + n, net.peer(dk=dk, dz=dz)
+        )
+    acc = tok[...]
+    for n in range(7):
+        net.landed(tok_one.at[n], tok_site + n)
+        acc = acc + tok_one[n]
+    tok_sum[...] = acc
+    for n, (dy, dz) in enumerate(others):
+        net.send(tok_sum, tok_two.at[n], tok_site + 7 + n, net.peer(dy=dy, dz=dz))
+    for one_sum in sums:
+        one_sum.hand_out()
+    for one_sum in sums:
+        one_sum.share()
+    for n in range(3):
+        net.landed(tok_two.at[n], tok_site + 7 + n)
+        acc = acc + tok_two[n]
+    out_tok[...] = acc
+    for n, flip in enumerate((1, 2, 3)):
+        net.landed(out_small.at[net.slice ^ flip], small_site + 3 + n)
+    for one_sum in sums:
+        one_sum.finish()
+    out_ready(res_out, res_site)
+    out_ready(grad_out, grad_site)
+    net.drain()
+    sems.append(net.used)
+
+
+def layer_on_square(
+    inputs, cotangent, seg_parent, token_depth, ln1_gain, ln1_bias, w_qkv, b_qv, w_out, b_out,
+    ln2_gain, ln2_bias, w_up, b_up, w_down, b_down,
+):
+    half_tokens, quarter = inputs.shape
+    tokens, width = token_depth.shape[0], 4 * quarter
+    shard = tokens // 8
+    head = HD
+    slices = w_qkv.shape[2] // head
+    hidden = w_up.shape[1] // slices
+    row = lax.axis_index("row")
+
+    seg_len = tokens // 16
+    parent = seg_parent - lax.axis_index("dp") * seg_parent.shape[0]
+    seg = jnp.maximum(jnp.arange(16, dtype=jnp.int32) - 3, 0)
+    key_seg = jnp.repeat(seg, seg_len)
+    ids = jnp.arange(seg_parent.shape[0], dtype=jnp.int32)
+    up_one = jnp.sum(jnp.where(seg[:, None] == ids[None, :], parent[None, :], 0), axis=1)
+    up_two = jnp.sum(jnp.where(up_one[:, None] == ids[None, :], parent[None, :], 0), axis=1)
+    keys = key_seg[None, :]
+    allowed = (keys == seg[:, None]) | (keys == up_one[:, None]) | (keys == up_two[:, None])
+    table = jnp.where(allowed, token_depth[None, :].astype(F32), -1.0)
+
+    w_q = w_qkv.reshape(quarter, 3, slices, head).transpose(2, 0, 1, 3)
+    w_q = w_q.reshape(slices, quarter, 3 * head)
+    blank = jnp.zeros_like(ln1_gain)
+    vectors = jnp.stack([ln1_gain, ln1_bias, b_out, ln2_gain, ln2_bias, b_down, blank, blank])
+
+    any_ = pl.BlockSpec(memory_space=pl.ANY)
+    vmem = pl.BlockSpec(memory_space=pltpu.VMEM)
+    sds = jax.ShapeDtypeStruct
+
+    def vm(*dims, dtype=BF):
+        return pltpu.VMEM(dims, dtype)
+
+    blocks = {"q": (quarter, 3 * head), "o": (head, quarter), "d": (hidden, quarter), "u": (quarter, hidden)}
+    names = ("q", "o", "d", "u")
+    scratch = [
+        vm(shard, width),
+        *[vm(8, shard, width) for _ in range(4)],
+        vm(width, 3 * head), vm(head, width), vm(hidden, width), vm(width, hidden),
+        vm(16, tokens, dtype=F32), vm(8, width, dtype=F32), vm(16, tokens, dtype=F32),
+        *[vm(tokens, head) for _ in range(3)], vm(tokens, tokens),
+        vm(tokens, head, dtype=F32), vm(tokens, head),
+        vm(8, shard, width), vm(8, shard, width), vm(3, shard, width), vm(3, shard, width),
+        vm(4, 4, shard, width), vm(4, 3, shard, width),
+        vm(tokens, hidden, dtype=F32), vm(tokens, hidden), vm(tokens, hidden),
+        vm(tokens, head), vm(tokens, head, dtype=F32), vm(tokens, head, dtype=F32),
+        vm(tokens, 3 * head),
+        vm(shard, width, dtype=F32), vm(shard, width, dtype=F32), vm(shard, width), vm(shard, width),
+        *[vm(2, 2, *blocks[n]) for n in names],
+        *[vm(2, *blocks[n]) for n in names],
+        *[vm(*blocks[n]) for n in names],
+        *[vm(*blocks[n]) for n in names],
+        *[vm(*blocks[n]) for n in names],
+        vm(8, width, dtype=F32), vm(7, 8, width, dtype=F32), vm(8, width, dtype=F32),
+        vm(3, 8, width, dtype=F32),
+        vm(8, hidden, dtype=F32), vm(3, 8, hidden, dtype=F32), vm(8, hidden, dtype=F32),
+        pltpu.SemaphoreType.DMA((180,)), pltpu.SemaphoreType.DMA((180,)),
+        pltpu.SemaphoreType.DMA((4,)),
+    ]
+    used = []
+    outs = pl.pallas_call(
+        functools.partial(layer_kernel, EPS, MASKED, used),
+        out_shape=(
+            sds((half_tokens, quarter), BF), sds((half_tokens, quarter), BF),
+            *[sds((slices, *blocks[n]), BF) for n in names],
+            sds((8, width), F32), sds((slices, 8, hidden), F32),
+        ),
+        in_specs=[any_] * 6 + [vmem] * 4,
+        out_specs=(any_,) * 6 + (vmem,) * 2,
+        scratch_shapes=scratch,
+        compiler_params=pltpu.CompilerParams(
+            collective_id=0, has_side_effects=True, vmem_limit_bytes=60 << 20
+        ),
+        name="tree_layer",
+    )(
+        inputs, cotangent, w_q, w_out, w_down, w_up, table, vectors,
+        b_up.reshape(1, -1), b_qv,
+    )
+    result, input_grad, g_q, g_o, g_u, g_d, by_token, small = (
+        outs[0], outs[1], outs[2], outs[3], outs[5], outs[4], outs[6], outs[7],
+    )
+    by_token = lax.dynamic_slice_in_dim(by_token, row * quarter, quarter, 1)
+    grad_w_qkv = g_q.reshape(slices, quarter, 3, head).transpose(1, 2, 0, 3)
+    grad_w_qkv = grad_w_qkv.reshape(quarter, 3, slices * head).astype(F32)
+    grad_w_up = g_u.transpose(1, 0, 2).reshape(quarter, slices * hidden).astype(F32)
+    grad_b_qv = jnp.stack(
+        [small[:, 1, :head].reshape(-1), small[:, 1, head : 2 * head].reshape(-1)]
+    )
+    return (
+        result.astype(F32),
+        input_grad.astype(F32),
+        by_token[0],
+        by_token[1],
+        grad_w_qkv,
+        grad_b_qv,
+        g_o.reshape(slices * head, quarter).astype(F32),
+        by_token[4],
+        by_token[2],
+        by_token[3],
+        grad_w_up,
+        small[:, 0].reshape(-1),
+        g_d.reshape(slices * hidden, quarter).astype(F32),
+        by_token[5],
+    )
+
+
+def fits_square(mesh, *arrays):
+    sizes = tuple(mesh.shape[name] for name in ("dp", "row", "col"))
+    return (
+        sizes == (4, 4, 2)
+        and arrays[0].shape == (512, 256)
+        and arrays[2].shape == (13,)
+        and arrays[3].shape == (1024,)
+        and arrays[6].shape == (256, 3, 512)
+        and arrays[12].shape == (256, 2048)
+    )
+
+
 def solution(mesh):
     placed = (
         P(("dp", "col"), "row"),
@@ -353,8 +1134,12 @@
         P("col", "row"),
         P("row"),
     )
+
+    def on_each(*arrays):
+        return (layer_on_square if fits_square(mesh, *arrays) else on_device)(*arrays)
+
     return jax.shard_map(
-        on_device,
+        on_each,
         mesh=mesh,
         in_specs=placed,
         out_specs=(

time: 1130 us -> 258 us (0.23)
  the two profiles are of different devices: /device:TPU:0 before, /device:TPU:9 now
where the time goes in v1:
time: 258 us; the launch traced here: 257 us
  Pallas kernels  234 us (91%)
  local copies, waits for them, and re-layouts  14 us (5%)
  other arithmetic  8.59 us (3%)
    pallas_call x1, Pallas kernels, layer_on_square(): pl.pallas_call(functools.partial(layer_kernel, EPS, MASKED, used), out_sh...  234 us
    unnamed x25, local copies, waits for them, and re-layouts  6.08 us

profile of v1, /device:TPU:9, one launch (start us, length us, event | category | flops | bytes accessed | tf_op | source)
XLA Modules:
  0.0 257.3 jit_solution(8875179171766402662)
XLA Ops:
  0.7 0.7 broadcast_subtract_fusion
  1.3 0.2 select_reduce_fusion.1
  1.5 0.2 select_reduce_fusion
  1.7 0.1 broadcast_in_dim.45
  1.8 0.1 eq.71
  1.8 0.7 convert_element_type.43
  2.5 0.7 or_select_fusion.refs_6_
  3.3 0.0 copy-start.9
  3.3 0.0 copy-start.10
  3.3 1.5 copy.44
  4.7 0.1 copy.45
  4.8 1.2 copy.46.refs_2_
  6.0 0.0 copy-done.5
  6.0 0.0 copy-done.6
  6.0 0.0 copy-done.7
  6.0 0.6 stack.34.refs_7_
  6.6 233.9 %tree_layer.1 = (bf16[512,256]{1,0:T(8,128)(2,1)}, bf16[512,256]{1,0:T(8,128)(2,1)}, bf16[4,256,384]{2,1,0:T(8,128)(2,1)}, bf16[4,128,256]{2,1,0:T(8,128)(2,1)},...) custom-call(bf16[512,256]{1,0:T(8,128)(2,1)} %refs_0_.1, ...), custom_call_target="tpu_custom_call" | custom-call | tf_op jit(solution)/shard_map/tree_layer/pallas_call | solution.py:1060
  240.6 0.7 slice_bitcast_fusion.1
  241.3 0.6 pad_maximum_fusion
  241.9 1.6 fusion
  243.5 1.4 slice.34
  244.9 1.5 convert_bitcast_fusion
  246.4 1.8 copy.49
  248.2 3.0 %copy.51 = f32[256,2048]{1,0:T(8,128)} copy(f32[256,2048]{0,1:T(8,128)} %bitcast.35) | data formatting | bytes 4194304
  251.2 0.3 copy.47
  251.5 0.1 copy.48
  251.6 0.0 copy-start
  251.6 1.6 copy.50
  253.2 1.5 bitcast_convert_fusion
  254.8 0.8 bitcast_convert_fusion.1
  255.6 0.8 convert_element_type.44
  256.4 0.8 convert_element_type.45
  (18 shorter events, 0.0 us)
Async XLA Ops:
  3.2 2.7 %copy-start.5 = (f32[256]{0:T(256)S(1)}, f32[256]{0:T(256)}, u32[]{:S(2)}) copy-start(f32[256]{0:T(256)} %param.20) | copy-start | bytes 3076
  3.2 2.7 %copy-start.6 = (f32[256]{0:T(256)S(1)}, f32[256]{0:T(256)}, u32[]{:S(2)}) copy-start(f32[256]{0:T(256)} %param.21) | copy-start | bytes 3076
  3.2 2.7 %copy-start.7 = (f32[256]{0:T(256)S(1)}, f32[256]{0:T(256)}, u32[]{:S(2)}) copy-start(f32[256]{0:T(256)} %param.25) | copy-start | bytes 3076
  3.2 2.7 %copy-start.8 = (f32[256]{0:T(256)S(1)}, f32[256]{0:T(256)}, u32[]{:S(2)}) copy-start(f32[256]{0:T(256)} %param.26) | copy-start | bytes 3076
  3.3 2.7 %copy-start.9 = (f32[256]{0:T(256)S(1)}, f32[256]{0:T(256)}, u32[]{:S(2)}) copy-start(f32[256]{0:T(256)} %param.27) | copy-start | bytes 3076
  3.3 2.7 %copy-start.10 = (f32[256]{0:T(256)S(1)}, f32[256]{0:T(256)}, u32[]{:S(2)}) copy-start(f32[256]{0:T(256)} %param.31) | copy-start | bytes 3076
  248.2 3.0 %copy-start.1 = (bf16[4,256,384]{2,1,0:T(8,128)(2,1)S(1)}, bf16[4,256,384]{2,1,0:T(8,128)(2,1)}, u32[]{:S(2)}) copy-start(bf16[4,256,384]{2,1,0:T(8,128)(2,1)} %get-tuple-element.25) | copy-start | bytes 2359300
  251.6 1.6 copy-start
  253.2 1.6 copy-start.4
  253.2 2.4 copy-start.3
  253.2 3.2 %copy-start.2 = (bf16[512,256]{1,0:T(8,128)(2,1)S(1)}, bf16[512,256]{1,0:T(8,128)(2,1)}, u32[]{:S(2)}) copy-start(bf16[512,256]{1,0:T(8,128)(2,1)} %get-tuple-element.23) | copy-start | bytes 786436

commit v2 on v1

--- a/solution.py
+++ b/solution.py
@@ -437,59 +437,84 @@
 
 
 class Gather:
-    def __init__(self, net, buf):
-        self.net, self.buf = net, buf
-        self.first = net.sites(7)
+    def __init__(self, net, buf, by_low, over_y=False):
+        self.net, self.buf, self.over_y = net, buf, over_y
+        self.slot = net.x * 4 + net.y * 2 + net.k if over_y else net.slot
+        self.first = net.sites(8)
+        rows = buf.shape[1]
+        self.low_rows = pl.ds(0, by_low) if by_low else None
+        self.x_rows = pl.ds(by_low, rows - by_low) if by_low < rows else None
+
+    def to(self, rel):
+        low = (rel >> 1) & 1
+        where = {"dy": low} if self.over_y else {"dz": low}
+        return self.net.peer(dk=rel & 1, dx=rel >> 2, **where)
 
     def start(self):
-        net, buf = self.net, self.buf
-        own = buf.at[net.slot]
-        net.send(own, own, self.first, net.rel(1))
-        for j in (1, 2, 3):
-            net.send(own, own, self.first + j, net.rel(RELS[j]))
+        own = self.buf.at[self.slot]
+        for n, rel in enumerate((1, 4, 2)):
+            self.net.send(own, own, self.first + n, self.to(rel))
 
     def relay(self, j):
-        net, buf = self.net, self.buf
-        part = buf.at[net.slot ^ RELS[j]]
-        net.landed(part, self.first + j)
-        net.send(part, part, self.first + 3 + j, net.rel(1))
+        net = self.net
+        part = self.buf.at[self.slot ^ RELS[j]]
+        if j < 3:
+            net.landed(part, self.first + j)
+            rows, rel = ((self.low_rows, 2), (self.x_rows, 4))[j - 1]
+            if rows is not None:
+                some = part.at[rows, :]
+                net.send(some, some, self.first + 2 + j, self.to(rel))
+        else:
+            for n, rows in enumerate((self.low_rows, self.x_rows)):
+                if rows is not None:
+                    net.landed(part.at[rows, :], self.first + 3 + n)
+        net.send(part, part, self.first + 4 + j, self.to(1))
 
     def ready(self, j):
-        net, buf = self.net, self.buf
-        part = buf.at[net.slot ^ RELS[j] ^ 1]
-        net.landed(part, self.first if j == 0 else self.first + 3 + j)
+        part = self.buf.at[self.slot ^ RELS[j] ^ 1]
+        self.net.landed(part, self.first if j == 0 else self.first + 4 + j)
 
     def block(self, j):
-        chip = self.net.chip ^ (RELS[j] >> 1)
+        chip = (self.slot ^ RELS[j]) // 2
         both = self.buf[pl.ds(chip * 2, 2)]
         return both.reshape(2 * both.shape[1], both.shape[2])
 
 
+class Exchange:
+    def __init__(self, net, src_of, dst_of):
+        self.net, self.src_of, self.dst_of = net, src_of, dst_of
+        self.first = net.sites(7)
+
+    def start(self):
+        net = self.net
+        for n in (6, 7, 4, 5, 2, 3, 1):
+            net.send(
+                self.src_of(net.slot ^ n), self.dst_of(net.slot), self.first + n - 1, net.rel(n)
+            )
+
+    def ready(self):
+        net = self.net
+        for n in range(1, 8):
+            net.landed(self.dst_of(net.slot ^ n), self.first + n - 1)
+
+
 class Scatter:
-    def __init__(self, net, part, hop, land_one, land_two):
-        self.net, self.part, self.hop_buf = net, part, hop
-        self.one, self.two = land_one, land_two
-        self.first = net.sites(7)
+    def __init__(self, net, bufs, land):
+        self.net = net
+        self.part, self.hops, self.kept, self.last = bufs
+        self.one, self.two, self.three = land
+        self.first = net.sites(10)
         self.sent = []
+
+    def send(self, src, dst, site, rel):
+        self.sent.append(self.net.send(src, dst, self.first + site, self.net.rel(rel)))
 
     def put(self, j, value):
         net = self.net
         chip = net.chip ^ (RELS[j] >> 1)
         shard = self.part.shape[1]
         self.part[pl.ds(chip * 2, 2)] = value.astype(BF).reshape(2, shard, value.shape[1])
-        self.push(j)
-
-    def push(self, j):
-        net = self.net
-        chip = net.chip ^ (RELS[j] >> 1)
-        self.sent.append(
-            net.send(
-                self.part.at[chip * 2 + (1 - net.k)],
-                self.one.at[j],
-                self.first + j,
-                net.rel(1),
-            )
-        )
+        self.send(self.part.at[chip * 2 + (1 - net.k)], self.one.at[j], j, 1)
 
     def chip_sum(self, j):
         net = self.net
@@ -498,16 +523,27 @@
         return self.part[chip * 2 + net.k].astype(F32) + self.one[j].astype(F32)
 
     def hop(self, j):
+        half = self.part.shape[1] // 2
+        value = self.chip_sum(j)
+        if j == 2:
+            self.kept[0] = value[:half]
+        else:
+            n = 0 if j == 1 else 1
+            self.hops[n] = value[:half].astype(BF)
+            self.send(self.hops.at[n], self.two.at[n], 4 + n, 4)
+        if j == 1:
+            self.kept[1] = value[half:]
+        else:
+            n = 2 if j == 2 else 3
+            self.hops[n] = value[half:].astype(BF)
+            self.send(self.hops.at[n], self.two.at[n], 4 + n, 2)
+
+    def hop_on(self):
         net = self.net
-        self.hop_buf[j - 1] = self.chip_sum(j).astype(BF)
-        self.sent.append(
-            net.send(
-                self.hop_buf.at[j - 1],
-                self.two.at[j - 1],
-                self.first + 3 + j,
-                net.rel(RELS[j]),
-            )
-        )
+        for n, rel in enumerate((2, 4)):
+            net.landed(self.two.at[1 + 2 * n], self.first + 5 + 2 * n)
+            self.last[n] = (self.kept[n] + self.two[1 + 2 * n].astype(F32)).astype(BF)
+            self.send(self.last.at[n], self.three.at[n], 8 + n, rel)
 
     def left(self):
         for remote in self.sent:
@@ -518,71 +554,89 @@
     def total(self):
         net = self.net
         value = self.chip_sum(0)
-        for j in (1, 2, 3):
-            net.landed(self.two.at[j - 1], self.first + 3 + j)
-            value = value + self.two[j - 1].astype(F32)
-        return value
+        half = value.shape[0] // 2
+        parts = []
+        for n in (0, 1):
+            net.landed(self.two.at[2 * n], self.first + 4 + 2 * n)
+            net.landed(self.three.at[n], self.first + 8 + n)
+            parts.append(
+                value[n * half : (n + 1) * half]
+                + self.two[2 * n].astype(F32)
+                + self.three[n].astype(F32)
+            )
+        return jnp.concatenate(parts, axis=0)
 
 
 class TreeSum:
-    def __init__(self, net, own, land_y, hop, land_z, done, out):
+    def __init__(self, net, own, land_y, hop, land_z, done, out, local_sem):
         self.net, self.own, self.land_y = net, own, land_y
         self.hop_buf, self.land_z, self.done, self.out = hop, land_z, done, out
-        self.first = net.sites(8)
+        self.first = net.sites(7)
+        self.local_sem = local_sem
+
+    def put(self, z, value):
+        rows = self.own.shape[3]
+        self.own[z // 2, z % 2] = value.astype(BF).reshape(2, rows, value.shape[1])
+
+    def half(self, piece, which):
+        return self.out.at[piece, span(which, self.own.shape[3]), :]
 
     def start(self):
         net = self.net
-        net.send(self.own.at[:, 1 - net.y], self.land_y, self.first, net.peer(dy=1))
+        net.send(self.own.at[:, :, 1 - net.y], self.land_y, self.first, net.peer(dy=1))
 
     def across(self):
         net = self.net
         net.landed(self.land_y, self.first)
         far = 1 - net.zh
-        self.hop_buf[...] = (
-            self.own[far, net.y].astype(F32) + self.land_y[far].astype(F32)
-        ).astype(BF)
+        for low in (0, 1):
+            self.hop_buf[low] = (
+                self.own[far, low, net.y].astype(F32) + self.land_y[far, low].astype(F32)
+            ).astype(BF)
         net.send(self.hop_buf, self.land_z, self.first + 1, net.peer(dz=2))
 
     def hand_out(self):
         net = self.net
         net.landed(self.land_z, self.first + 1)
-        self.done[...] = (
-            self.own[net.zh, net.y].astype(F32)
-            + self.land_y[net.zh].astype(F32)
-            + self.land_z[...].astype(F32)
-        ).astype(BF)
-        place = self.out.at[net.slice]
-        target = net.zh * 2 + net.y
-        for step in (0, 1):
-            net.send(
-                self.done,
-                place,
-                self.first + 2 + step,
-                ((net.y ^ step) * 2 + net.k, target, net.col),
-                recv_site=self.first + 4 + net.zl,
-                skip=(target == net.row) if step == 0 else None,
-            )
+        for low in (0, 1):
+            self.done[low] = (
+                self.own[net.zh, low, net.y].astype(F32)
+                + self.land_y[net.zh, low].astype(F32)
+                + self.land_z[low].astype(F32)
+            ).astype(BF)
+        place = self.half(net.slice, net.y)
+        net.send(self.done.at[1 - net.zl], place, self.first + 2, net.peer(dz=1))
+        net.send(self.done.at[net.zl], place, self.first + 3, net.peer(dy=1))
+        self.kept = pltpu.make_async_copy(self.done.at[net.zl], place, self.local_sem)
+        self.kept.start()
+
+    def pass_on(self):
+        net = self.net
+        part = self.half(net.slice ^ 2, net.y)
+        net.landed(part, self.first + 2)
+        net.send(part, part, self.first + 4, net.peer(dy=1))
 
     def share(self):
         net = self.net
-        for low in (0, 1):
-            part = self.out.at[low * 2 + net.k]
-            net.landed(part, self.first + 4 + low)
-            net.send(part, part, self.first + 6 + low, net.rel(1))
+        self.kept.wait()
+        for n, piece in enumerate((net.slice, net.slice ^ 2)):
+            net.landed(self.half(piece, 1 - net.y), self.first + 3 + n)
+            part = self.out.at[piece]
+            net.send(part, part, self.first + 5 + n, net.rel(1))
 
     def finish(self):
         net = self.net
-        for low in (0, 1):
-            net.landed(self.out.at[low * 2 + (1 - net.k)], self.first + 6 + low)
+        for n, piece in enumerate((net.slice ^ 1, net.slice ^ 3)):
+            net.landed(self.out.at[piece], self.first + 5 + n)
 
 
 def layer_kernel(eps, masked, sems, *refs):
     (
         inp, cot, w_q, w_o, w_d, w_u, tab, vec_in, b_up, b_qv,
         res_out, grad_out, out_q, out_o, out_d, out_u, out_tok, out_small,
-        xs, e1, g, e2, gb, wq, wo, wd, wu, tab_far, vec, bias,
+        xs, e1, g, e2, gb, wf, wq, wd, wu, mixed_all, grad_all, tab_far, vec, bias,
         q_buf, k_buf, v_buf, p_buf, mix, mix_b,
-        part_a, part_b, hop_a, hop_b, one, two,
+        part_a, hops_a, kept_a, last_a, part_b, hops_b, kept_b, last_b, one, two, three,
         gh, hid, gp, gm, dk_acc, dv_acc, dqkv, mid, gmid, back_a, back_b,
         dw_q, dw_o, dw_d, dw_u, ly_q, ly_o, ly_d, ly_u,
         yh_q, yh_o, yh_d, yh_u, lz_q, lz_o, lz_d, lz_u,
@@ -627,14 +681,11 @@
         for z in range(4):
             net.landed(dst.at[:, span(z, quarter)], first + 4 + z)
 
+    vec_site = net.sites(3)
+    for o in (1, 2, 3):
+        net.send(vec_in, vec.at[:, span(row, quarter)], vec_site + o - 1, net.peer(dz=o))
     home_x, home_g = net.sites(8), net.sites(8)
     send_home(inp, lambda s: xs, home_x)
-
-    vec_site = net.sites(3)
-    for o in (1, 2, 3):
-        net.send(
-            vec_in, vec.at[:, span(row, quarter)], vec_site + o - 1, net.peer(dz=o)
-        )
     tab_site = net.sites(1)
     net.send(tab, tab_far, tab_site, net.rel(1))
 
@@ -684,12 +735,18 @@
 
     hidden = hid.shape[1]
     weight_q = Weight(lambda s: w_q.at[s], wq, 0, 0)
-    weight_o = Weight(lambda s: w_o.at[span(s, head), :], wo, 1, 1)
     weight_d = Weight(lambda s: w_d.at[span(s, hidden), :], wd, 1, 2)
     weight_u = Weight(lambda s: w_u.at[:, span(s, hidden)], wu, 0, 3)
     weight_q.start()
-    send_home(cot, lambda s: g.at[x * 4 + s], home_g)
-    weight_o.start()
+
+    gather_w = Gather(net, wf, shard // 2, over_y=True)
+    wf_own = wf.at[gather_w.slot]
+    wf_site = net.sites(3)
+    wf_src = w_o.at[span(y * 2 + k, shard), :]
+    wf_copy = pltpu.make_async_copy(wf_src, wf_own.at[:, span(row, quarter)], lsem.at[1])
+    wf_copy.start()
+    for o in (1, 2, 3):
+        net.send(wf_src, wf_own.at[:, span(row, quarter)], wf_site + o - 1, net.peer(dz=o))
 
     vec[:, span(row, quarter)] = vec_in[...]
     for o in (1, 2, 3):
@@ -704,13 +761,13 @@
     home_ready(xs, home_x)
     normed, _ = norm_stats(xs[...].astype(F32))
     e1[net.slot] = (normed * vec[0:1, :] + vec[1:2, :]).astype(BF)
-    gather_e1 = Gather(net, e1)
+    gather_e1 = Gather(net, e1, 0)
     gather_e1.start()
-    gather_g = Gather(net, g)
+    gather_g = Gather(net, g, 0)
+    send_home(cot, lambda s: g.at[x * 4 + s], home_g)
+    weight_u.start()
     weight_d.start()
-    weight_u.start()
     weight_q.relay()
-    home_ready(g.at[net.slot], home_g)
 
     net.landed(tab_far, tab_site)
     table = jnp.where(zh == k, tab[...], tab_far[...])
@@ -720,19 +777,22 @@
 
     b_q = b_qv[0:1, span(net.slice, head)]
     b_v = b_qv[1:2, span(net.slice, head)]
+    gather_e1.relay(1)
+    gather_e1.relay(2)
     weight_q.ready()
     for j in range(4):
-        if j:
-            gather_e1.relay(j)
         if j == 3:
-            gather_g.start()
+            for o in (1, 2, 3):
+                net.landed(wf_own.at[:, span(row ^ o, quarter)], wf_site + o - 1)
+            wf_copy.wait()
+            gather_w.start()
+            gather_e1.relay(3)
         gather_e1.ready(j)
-        rows = span(net.chip ^ (RELS[j] >> 1), 2 * shard)
+        rows = pl.ds((net.chip ^ (RELS[j] >> 1)) * 2 * shard, 2 * shard)
         proj = dot_nn(gather_e1.block(j), wq[...])
         q_buf[rows, :] = (proj[:, :head] + b_q).astype(BF)
         k_buf[rows, :] = proj[:, head : 2 * head].astype(BF)
         v_buf[rows, :] = (proj[:, 2 * head :] + b_v).astype(BF)
-    weight_o.relay()
 
     scale = head ** (-0.5)
     seg_len = tokens // 16
@@ -762,28 +822,50 @@
         mix_b[pl.ds(first, shard), :] = mixed.astype(BF)
         return carry
 
-    lax.fori_loop(0, 8, attend, 0)
-
-    for j in (1, 2, 3):
-        gather_g.relay(j)
-    weight_o.ready()
+    lax.fori_loop(0, 6, attend, 0)
+    gather_w.relay(1)
+    gather_w.relay(2)
+    lax.fori_loop(6, 8, attend, 0)
 
     def rows_of(j):
         return span(net.chip ^ (RELS[j] >> 1), 2 * shard)
 
     order = (3, 1, 2, 0)
-    scatter = Scatter(net, part_a, hop_a, one.at[0], two.at[0])
-    for j in order:
-        scatter.put(j, dot_nn(mix_b[rows_of(j), :], wo[...]))
-    for j in (3, 1, 2):
-        scatter.hop(j)
+    part_set_a = (part_a, hops_a, kept_a, last_a)
+    part_set_b = (part_b, hops_b, kept_b, last_b)
+
+    def landings(n):
+        return (one.at[n], two.at[n], three.at[n])
+
+    swap = Exchange(
+        net, lambda q: mix_b.at[span(q, shard), :], lambda h: mixed_all.at[:, span(h, head)]
+    )
+    swap.start()
+    mixed_all[:, span(net.slot, head)] = mix_b[span(net.slot, shard), :]
+    home_ready(g.at[net.slot], home_g)
+    gather_g.start()
+    gather_w.relay(3)
+    weight_u.relay()
+    for j in range(4):
+        gather_w.ready(j)
+    swap.ready()
+    w_out = wf[...].reshape(width, width)
+
+    middle = xs[...].astype(F32) + dot_nn(mixed_all[...], w_out) + vec[2:3, :]
+    mid[...] = middle
+    normed, _ = norm_stats(middle)
+    e2[net.slot] = (normed * vec[3:4, :] + vec[4:5, :]).astype(BF)
+    gather_e2 = Gather(net, e2, shard // 2)
+    gather_e2.start()
     weight_d.relay()
-    weight_u.relay()
+    gather_g.relay(1)
+    gather_g.relay(2)
+    gather_e2.relay(1)
+    gather_e2.relay(2)
+    gather_g.relay(3)
     weight_d.ready()
-    gather_g.ready(0)
-    gather_g.ready(1)
-    gather_g.ready(2)
-    gather_g.ready(3)
+    for j in range(4):
+        gather_g.ready(j)
 
     def hidden_grad(c, carry):
         rows = span(c, 2 * shard)
@@ -793,20 +875,12 @@
 
     lax.fori_loop(0, 4, hidden_grad, 0)
 
-    middle = xs[...].astype(F32) + scatter.total() + vec[2:3, :]
-    mid[...] = middle
-    normed, _ = norm_stats(middle)
-    e2[net.slot] = (normed * vec[3:4, :] + vec[4:5, :]).astype(BF)
-    gather_e2 = Gather(net, e2)
-    gather_e2.start()
-    scatter.left()
-
     b_u = b_up[0:1, span(net.slice, hidden)]
     weight_u.ready()
-    scatter_two = Scatter(net, part_a, hop_a, one.at[1], two.at[1])
+    scatter_two = Scatter(net, part_set_a, landings(0))
     for j in range(4):
-        if j:
-            gather_e2.relay(j)
+        if j == 3:
+            gather_e2.relay(3)
         gather_e2.ready(j)
         pre = dot_nn(gather_e2.block(j), wu[...]) + b_u
         bell = 0.5 * (1.0 + lax.erf(pre * (1.0 / math.sqrt(2.0))))
@@ -814,25 +888,34 @@
         rise = bell + pre * jnp.exp(-0.5 * pre * pre) * (1.0 / math.sqrt(2.0 * math.pi))
         gp[rows_of(j), :] = (gh[rows_of(j), :] * rise).astype(BF)
         scatter_two.put(j, dot_nt(gp[rows_of(j), :], wu[...]))
-        if j > 1:
-            scatter_two.hop(j - 1)
+        if j == 2:
+            scatter_two.hop(1)
+    scatter_two.hop(2)
     scatter_two.hop(3)
 
-    sum_d = TreeSum(net, dw_d, ly_d, yh_d, lz_d, fin_d, out_d)
-    sum_u = TreeSum(net, dw_u, ly_u, yh_u, lz_u, fin_u, out_u)
-    sum_o = TreeSum(net, dw_o, ly_o, yh_o, lz_o, fin_o, out_o)
-    sum_q = TreeSum(net, dw_q, ly_q, yh_q, lz_q, fin_q, out_q)
+    sum_d = TreeSum(net, dw_d, ly_d, yh_d, lz_d, fin_d, out_d, lsem.at[4])
+    sum_u = TreeSum(net, dw_u, ly_u, yh_u, lz_u, fin_u, out_u, lsem.at[5])
+    sum_o = TreeSum(net, dw_o, ly_o, yh_o, lz_o, fin_o, out_o, lsem.at[6])
+    sum_q = TreeSum(net, dw_q, ly_q, yh_q, lz_q, fin_q, out_q, lsem.at[7])
 
     def columns(buf, z):
         part = buf[:, :, span(z, quarter)]
         return part.reshape(tokens, quarter)
 
     def grad_down(z, carry):
-        dw_d[z // 2, z % 2] = dot_tn(hid[...], columns(g, z)).astype(BF)
+        sum_d.put(z, dot_tn(hid[...], columns(g, z)))
         return carry
 
     lax.fori_loop(0, 4, grad_down, 0)
     sum_d.start()
+    scatter_two.hop_on()
+
+    def grad_up(z, carry):
+        sum_u.put(z, dot_tn(columns(e2, z), gp[...]))
+        return carry
+
+    lax.fori_loop(0, 4, grad_up, 0)
+    sum_u.start()
 
     grad = scatter_two.total()
     middle = mid[...]
@@ -850,12 +933,14 @@
     gb[net.slot] = branch
     tok[4:5, :] = jnp.sum(branch.astype(F32), axis=0, keepdims=True)
     tok[6:8, :] = jnp.zeros((2, width), F32)
-    gather_gb = Gather(net, gb)
+    grad_all[...] = dot_nt(branch, w_out).astype(BF)
+    swap_back = Exchange(
+        net, lambda h: grad_all.at[:, span(h, head)], lambda q: gm.at[span(q, shard), :]
+    )
+    swap_back.start()
+    gm[span(net.slot, shard), :] = grad_all[:, span(net.slot, head)]
+    gather_gb = Gather(net, gb, shard // 2)
     gather_gb.start()
-
-    scatter_three = Scatter(net, part_b, hop_b, one.at[2], two.at[2])
-    for j in order:
-        scatter_three.put(j, dot_nn(hid[rows_of(j), :], wd[...]))
 
     dk_acc[...] = jnp.zeros_like(dk_acc)
     dv_acc[...] = jnp.zeros_like(dv_acc)
@@ -871,50 +956,35 @@
         dk_acc[...] += dot_tn(grad_scores, q_buf[rows, :])
         dv_acc[...] += dot_tn(probs, grad_mix)
 
-    for j in range(4):
-        if j:
-            gather_gb.relay(j)
-        gather_gb.ready(j)
-        chip = net.chip ^ (RELS[j] >> 1)
-        gm[rows_of(j), :] = dot_nt(gather_gb.block(j), wo[...]).astype(BF)
-
-        def two_tiles(t, carry, chip=chip):
-            attend_back(pl.multiple_of((chip * 2 + t) * shard, shard))
-            return carry
-
-        lax.fori_loop(0, 2, two_tiles, 0)
+    swap_back.ready()
+
+    def tile_back(t, carry):
+        attend_back(pl.multiple_of(t * shard, shard))
+        return carry
+
+    lax.fori_loop(0, 5, tile_back, 0)
+    gather_gb.relay(1)
+    gather_gb.relay(2)
+    lax.fori_loop(5, 8, tile_back, 0)
     dqkv[:, head : 2 * head] = (dk_acc[...] * scale).astype(BF)
     dqkv[:, 2 * head :] = dv_acc[...].astype(BF)
 
-    for j in (3, 1, 2):
-        scatter_three.hop(j)
+    scatter_four = Scatter(net, part_set_a, landings(1))
     scatter_two.left()
-    scatter_four = Scatter(net, part_a, hop_a, one.at[3], two.at[3])
     for j in order:
         scatter_four.put(j, dot_nt(dqkv[rows_of(j), :], wq[...]))
     for j in (3, 1, 2):
         scatter_four.hop(j)
+    sum_d.across()
 
     def grad_qkv(z, carry):
-        dw_q[z // 2, z % 2] = dot_tn(columns(e1, z), dqkv[...]).astype(BF)
+        sum_q.put(z, dot_tn(columns(e1, z), dqkv[...]))
         return carry
 
     lax.fori_loop(0, 4, grad_qkv, 0)
     sum_q.start()
-
-    def grad_up(z, carry):
-        dw_u[z // 2, z % 2] = dot_tn(columns(e2, z), gp[...]).astype(BF)
-        return carry
-
-    lax.fori_loop(0, 4, grad_up, 0)
-    sum_u.start()
-
-    def grad_o(z, carry):
-        dw_o[z // 2, z % 2] = dot_tn(mix_b[...], columns(gb, z)).astype(BF)
-        return carry
-
-    lax.fori_loop(0, 4, grad_o, 0)
-    sum_o.start()
+    scatter_four.hop_on()
+    sum_u.across()
 
     small[...] = jnp.zeros_like(small)
     small[0:1, :] = jnp.sum(gp[...].astype(F32), axis=0, keepdims=True)
@@ -941,9 +1011,6 @@
             net.landed(dst.at[span(s, shard), :], first + 4 + s)
 
     res_site, grad_site = net.sites(8), net.sites(8)
-    back_a[...] = (mid[...] + scatter_three.total() + vec[5:6, :]).astype(BF)
-    send_out(back_a, res_out, res_site)
-
     grad = scatter_four.total()
     normed, inv = norm_stats(xs[...].astype(F32))
     tok[0:1, :] = jnp.sum(grad * normed, axis=0, keepdims=True)
@@ -957,9 +1024,30 @@
     back_b[...] = (gmid[...] + inv * (spread - mean_one - normed * mean_two)).astype(BF)
     send_out(back_b, grad_out, grad_site)
 
-    sums = (sum_d, sum_q, sum_u, sum_o)
-    for one_sum in sums:
-        one_sum.across()
+    sum_d.hand_out()
+    sum_q.across()
+    gather_gb.relay(3)
+    for j in range(4):
+        gather_gb.ready(j)
+
+    def grad_o(z, carry):
+        sum_o.put(z, dot_tn(mix_b[...], columns(gb, z)))
+        return carry
+
+    lax.fori_loop(0, 4, grad_o, 0)
+    sum_o.start()
+    scatter_three = Scatter(net, part_set_b, landings(2))
+    for j in order:
+        scatter_three.put(j, dot_nn(hid[rows_of(j), :], wd[...]))
+    for j in (3, 1, 2):
+        scatter_three.hop(j)
+    sum_u.hand_out()
+    sum_d.pass_on()
+    sum_o.across()
+    scatter_three.hop_on()
+    sum_q.hand_out()
+    sum_u.pass_on()
+    sum_d.share()
     acc = small[...]
     for n in range(3):
         net.landed(small_land.at[n], small_site + n)
@@ -977,17 +1065,21 @@
     tok_sum[...] = acc
     for n, (dy, dz) in enumerate(others):
         net.send(tok_sum, tok_two.at[n], tok_site + 7 + n, net.peer(dy=dy, dz=dz))
-    for one_sum in sums:
-        one_sum.hand_out()
-    for one_sum in sums:
-        one_sum.share()
+    sum_o.hand_out()
+    sum_q.pass_on()
+    sum_u.share()
+    sum_o.pass_on()
+    back_a[...] = (mid[...] + scatter_three.total() + vec[5:6, :]).astype(BF)
+    send_out(back_a, res_out, res_site)
+    sum_q.share()
+    sum_o.share()
     for n in range(3):
         net.landed(tok_two.at[n], tok_site + 7 + n)
         acc = acc + tok_two[n]
     out_tok[...] = acc
     for n, flip in enumerate((1, 2, 3)):
         net.landed(out_small.at[net.slice ^ flip], small_site + 3 + n)
-    for one_sum in sums:
+    for one_sum in (sum_d, sum_u, sum_q, sum_o):
         one_sum.finish()
     out_ready(res_out, res_site)
     out_ready(grad_out, grad_site)
@@ -1032,29 +1124,38 @@
 
     blocks = {"q": (quarter, 3 * head), "o": (head, quarter), "d": (hidden, quarter), "u": (quarter, hidden)}
     names = ("q", "o", "d", "u")
+    halves = {n: (blocks[n][0] // 2, blocks[n][1]) for n in names}
     scratch = [
         vm(shard, width),
-        *[vm(8, shard, width) for _ in range(4)],
-        vm(width, 3 * head), vm(head, width), vm(hidden, width), vm(width, hidden),
+        *[vm(8, shard, width) for _ in range(5)],
+        vm(width, 3 * head), vm(hidden, width), vm(width, hidden),
+        vm(shard, width), vm(shard, width),
         vm(16, tokens, dtype=F32), vm(8, width, dtype=F32), vm(16, tokens, dtype=F32),
         *[vm(tokens, head) for _ in range(3)], vm(tokens, tokens),
         vm(tokens, head, dtype=F32), vm(tokens, head),
-        vm(8, shard, width), vm(8, shard, width), vm(3, shard, width), vm(3, shard, width),
-        vm(4, 4, shard, width), vm(4, 3, shard, width),
+        *[
+            spec
+            for _ in range(2)
+            for spec in (
+                vm(8, shard, width), vm(4, shard // 2, width),
+                vm(2, shard // 2, width, dtype=F32), vm(2, shard // 2, width),
+            )
+        ],
+        vm(3, 4, shard, width), vm(3, 4, shard // 2, width), vm(3, 2, shard // 2, width),
         vm(tokens, hidden, dtype=F32), vm(tokens, hidden), vm(tokens, hidden),
         vm(tokens, head), vm(tokens, head, dtype=F32), vm(tokens, head, dtype=F32),
         vm(tokens, 3 * head),
         vm(shard, width, dtype=F32), vm(shard, width, dtype=F32), vm(shard, width), vm(shard, width),
-        *[vm(2, 2, *blocks[n]) for n in names],
-        *[vm(2, *blocks[n]) for n in names],
-        *[vm(*blocks[n]) for n in names],
-        *[vm(*blocks[n]) for n in names],
-        *[vm(*blocks[n]) for n in names],
+        *[vm(2, 2, 2, *halves[n]) for n in names],
+        *[vm(2, 2, *halves[n]) for n in names],
+        *[vm(2, *halves[n]) for n in names],
+        *[vm(2, *halves[n]) for n in names],
+        *[vm(2, *halves[n]) for n in names],
         vm(8, width, dtype=F32), vm(7, 8, width, dtype=F32), vm(8, width, dtype=F32),
         vm(3, 8, width, dtype=F32),
         vm(8, hidden, dtype=F32), vm(3, 8, hidden, dtype=F32), vm(8, hidden, dtype=F32),
-        pltpu.SemaphoreType.DMA((180,)), pltpu.SemaphoreType.DMA((180,)),
-        pltpu.SemaphoreType.DMA((4,)),
+        pltpu.SemaphoreType.DMA((200,)), pltpu.SemaphoreType.DMA((200,)),
+        pltpu.SemaphoreType.DMA((8,)),
     ]
     used = []
     outs = pl.pallas_call(

time: 258 us -> 197 us (0.76)
  the two profiles are of different devices: /device:TPU:9 before, /device:TPU:0 now
where the time goes in v2:
time: 197 us
  Pallas kernels  174 us (88%)
  local copies, waits for them, and re-layouts  14 us (7%)
  other arithmetic  8.59 us (4%)
    pallas_call x1, Pallas kernels, layer_on_square(): pl.pallas_call(functools.partial(layer_kernel, EPS, MASKED, used), out_sh...  174 us
    unnamed x25, local copies, waits for them, and re-layouts  6.08 us

profile of v2, /device:TPU:0, one launch (start us, length us, event | category | flops | bytes accessed | tf_op | source)
XLA Modules:
  0.0 196.9 jit_solution(692248119478420594)
XLA Ops:
  0.7 0.7 broadcast_subtract_fusion
  1.3 0.2 select_reduce_fusion.1
  1.5 0.2 select_reduce_fusion
  1.7 0.1 broadcast_in_dim.45
  1.8 0.1 eq.71
  1.8 0.7 convert_element_type.43
  2.5 0.7 or_select_fusion.refs_6_
  3.3 0.0 copy-start.9
  3.3 0.0 copy-start.10
  3.3 1.5 copy.44
  4.7 0.1 copy.45
  4.8 1.2 copy.46.refs_2_
  6.0 0.0 copy-done.5
  6.0 0.0 copy-done.6
  6.0 0.0 copy-done.7
  6.0 0.6 stack.34.refs_7_
  6.6 173.5 %tree_layer.1 = (bf16[512,256]{1,0:T(8,128)(2,1)}, bf16[512,256]{1,0:T(8,128)(2,1)}, bf16[4,256,384]{2,1,0:T(8,128)(2,1)}, bf16[4,128,256]{2,1,0:T(8,128)(2,1)},...) custom-call(bf16[512,256]{1,0:T(8,128)(2,1)} %refs_0_.1, ...), custom_call_target="tpu_custom_call" | custom-call | tf_op jit(solution)/shard_map/tree_layer/pallas_call | solution.py:1161
  180.2 0.7 slice_bitcast_fusion.1
  180.9 0.6 pad_maximum_fusion
  181.5 1.6 fusion
  183.1 1.4 slice.34
  184.5 1.5 convert_bitcast_fusion
  186.0 1.8 copy.49
  187.8 3.0 %copy.51 = f32[256,2048]{1,0:T(8,128)} copy(f32[256,2048]{0,1:T(8,128)} %bitcast.35) | data formatting | bytes 4194304
  190.8 0.3 copy.47
  191.1 0.1 copy.48
  191.2 1.6 copy.50
  192.8 0.0 copy-done
  192.8 1.5 bitcast_convert_fusion
  194.4 0.8 bitcast_convert_fusion.1
  195.2 0.8 convert_element_type.44
  196.0 0.8 convert_element_type.45
  (18 shorter events, 0.0 us)
Async XLA Ops:
  3.2 2.7 %copy-start.5 = (f32[256]{0:T(256)S(1)}, f32[256]{0:T(256)}, u32[]{:S(2)}) copy-start(f32[256]{0:T(256)} %param.20) | copy-start | bytes 3076
  3.2 2.7 %copy-start.6 = (f32[256]{0:T(256)S(1)}, f32[256]{0:T(256)}, u32[]{:S(2)}) copy-start(f32[256]{0:T(256)} %param.21) | copy-start | bytes 3076
  3.2 2.7 %copy-start.7 = (f32[256]{0:T(256)S(1)}, f32[256]{0:T(256)}, u32[]{:S(2)}) copy-start(f32[256]{0:T(256)} %param.25) | copy-start | bytes 3076
  3.2 2.7 %copy-start.8 = (f32[256]{0:T(256)S(1)}, f32[256]{0:T(256)}, u32[]{:S(2)}) copy-start(f32[256]{0:T(256)} %param.26) | copy-start | bytes 3076
  3.3 2.7 %copy-start.9 = (f32[256]{0:T(256)S(1)}, f32[256]{0:T(256)}, u32[]{:S(2)}) copy-start(f32[256]{0:T(256)} %param.27) | copy-start | bytes 3076
  3.3 2.7 %copy-start.10 = (f32[256]{0:T(256)S(1)}, f32[256]{0:T(256)}, u32[]{:S(2)}) copy-start(f32[256]{0:T(256)} %param.31) | copy-start | bytes 3076
  187.8 3.0 %copy-start.1 = (bf16[4,256,384]{2,1,0:T(8,128)(2,1)S(1)}, bf16[4,256,384]{2,1,0:T(8,128)(2,1)}, u32[]{:S(2)}) copy-start(bf16[4,256,384]{2,1,0:T(8,128)(2,1)} %get-tuple-element.25) | copy-start | bytes 2359300
  191.2 1.6 copy-start
  192.8 1.6 copy-start.4
  192.8 2.4 %copy-start.3 = (bf16[512,256]{1,0:T(8,128)(2,1)S(1)}, bf16[512,256]{1,0:T(8,128)(2,1)}, u32[]{:S(2)}) copy-start(bf16[512,256]{1,0:T(8,128)(2,1)} %get-tuple-element.22) | copy-start | bytes 786436
  192.8 3.2 %copy-start.2 = (bf16[512,256]{1,0:T(8,128)(2,1)S(1)}, bf16[512,256]{1,0:T(8,128)(2,1)}, u32[]{:S(2)}) copy-start(bf16[512,256]{1,0:T(8,128)(2,1)} %get-tuple-element.23) | copy-start | bytes 786436

commit v3 on v2

--- a/solution.py
+++ b/solution.py
@@ -499,12 +499,18 @@
 
 
 class Scatter:
-    def __init__(self, net, bufs, land):
-        self.net = net
+    def __init__(self, net, bufs, land, cut):
+        self.net, self.cut = net, cut
         self.part, self.hops, self.kept, self.last = bufs
         self.one, self.two, self.three = land
         self.first = net.sites(10)
         self.sent = []
+        rows = self.part.shape[1]
+        self.ways = [
+            way
+            for way in ((0, pl.ds(0, cut), 1, 2), (1, pl.ds(cut, rows - cut), 2, 1))
+            if way[1].size
+        ]
 
     def send(self, src, dst, site, rel):
         self.sent.append(self.net.send(src, dst, self.first + site, self.net.rel(rel)))
@@ -523,27 +529,29 @@
         return self.part[chip * 2 + net.k].astype(F32) + self.one[j].astype(F32)
 
     def hop(self, j):
-        half = self.part.shape[1] // 2
         value = self.chip_sum(j)
-        if j == 2:
-            self.kept[0] = value[:half]
-        else:
-            n = 0 if j == 1 else 1
-            self.hops[n] = value[:half].astype(BF)
-            self.send(self.hops.at[n], self.two.at[n], 4 + n, 4)
-        if j == 1:
-            self.kept[1] = value[half:]
-        else:
-            n = 2 if j == 2 else 3
-            self.hops[n] = value[half:].astype(BF)
-            self.send(self.hops.at[n], self.two.at[n], 4 + n, 2)
+        for n, rows, near, far in self.ways:
+            mine = value[rows.start : rows.start + rows.size]
+            if j == far:
+                self.kept[rows, :] = mine
+            else:
+                place = 0 if j == near else 1
+                self.hops[place, rows, :] = mine.astype(BF)
+                self.send(
+                    self.hops.at[place, rows, :],
+                    self.two.at[place, rows, :],
+                    4 + 2 * n + place,
+                    RELS[near],
+                )
 
     def hop_on(self):
         net = self.net
-        for n, rel in enumerate((2, 4)):
-            net.landed(self.two.at[1 + 2 * n], self.first + 5 + 2 * n)
-            self.last[n] = (self.kept[n] + self.two[1 + 2 * n].astype(F32)).astype(BF)
-            self.send(self.last.at[n], self.three.at[n], 8 + n, rel)
+        for n, rows, near, far in self.ways:
+            net.landed(self.two.at[1, rows, :], self.first + 5 + 2 * n)
+            self.last[rows, :] = (
+                self.kept[rows, :] + self.two[1, rows, :].astype(F32)
+            ).astype(BF)
+            self.send(self.last.at[rows, :], self.three.at[rows, :], 8 + n, RELS[far])
 
     def left(self):
         for remote in self.sent:
@@ -554,17 +562,10 @@
     def total(self):
         net = self.net
         value = self.chip_sum(0)
-        half = value.shape[0] // 2
-        parts = []
-        for n in (0, 1):
-            net.landed(self.two.at[2 * n], self.first + 4 + 2 * n)
-            net.landed(self.three.at[n], self.first + 8 + n)
-            parts.append(
-                value[n * half : (n + 1) * half]
-                + self.two[2 * n].astype(F32)
-                + self.three[n].astype(F32)
-            )
-        return jnp.concatenate(parts, axis=0)
+        for n, rows, near, far in self.ways:
+            net.landed(self.two.at[0, rows, :], self.first + 4 + 2 * n)
+            net.landed(self.three.at[rows, :], self.first + 8 + n)
+        return value + self.two[0].astype(F32) + self.three[...].astype(F32)
 
 
 class TreeSum:
@@ -630,17 +631,17 @@
             net.landed(self.out.at[piece], self.first + 5 + n)
 
 
-def layer_kernel(eps, masked, sems, *refs):
+def layer_kernel(eps, masked, used, *refs):
     (
-        inp, cot, w_q, w_o, w_d, w_u, tab, vec_in, b_up, b_qv,
-        res_out, grad_out, out_q, out_o, out_d, out_u, out_tok, out_small,
-        xs, e1, g, e2, gb, wf, wq, wd, wu, mixed_all, grad_all, tab_far, vec, bias,
+        inp, cot, w_q, w_o, w_d, w_u, vec_0, vec_1, vec_2, vec_3, vec_4, vec_5, parents, b_up, b_qv,
+        res_out, grad_out, out_a, out_b, out_o, out_d, out_u, out_tok, out_small,
+        xs, e1, g, e2, gb, wf, wq, wd, wu, mixed_all, grad_all, links, vec_in, vec, bias,
         q_buf, k_buf, v_buf, p_buf, mix, mix_b,
         part_a, hops_a, kept_a, last_a, part_b, hops_b, kept_b, last_b, one, two, three,
-        gh, hid, gp, gm, dk_acc, dv_acc, dqkv, mid, gmid, back_a, back_b,
-        dw_q, dw_o, dw_d, dw_u, ly_q, ly_o, ly_d, ly_u,
-        yh_q, yh_o, yh_d, yh_u, lz_q, lz_o, lz_d, lz_u,
-        fin_q, fin_o, fin_d, fin_u,
+        hid, gp, gm, dk_acc, dv_acc, dqkv, mid, gmid, back_a, back_b,
+        dw_a, dw_b, dw_o, dw_d, dw_u, ly_a, ly_b, ly_o, ly_d, ly_u,
+        yh_a, yh_b, yh_o, yh_d, yh_u, lz_a, lz_b, lz_o, lz_d, lz_u,
+        fin_a, fin_b, fin_o, fin_d, fin_u,
         tok, tok_one, tok_sum, tok_two, small, small_land, small_sum,
         ssem, rsem, lsem,
     ) = refs
@@ -659,6 +660,17 @@
         if dy + dk + dz
     ]
     greet += [net.peer(dk=dk, dz=dz, dx=1) for dk in (0, 1) for dz in (0, 1)]
+    vec_parts = (vec_0, vec_1, vec_2, vec_3, vec_4, vec_5)
+    for n, part in enumerate(vec_parts):
+        pltpu.make_async_copy(part, vec_in.at[pl.ds(n, 1), :], lsem.at[9]).start()
+    seg_count = parents.shape[0]
+    half_at = lax.broadcasted_iota(jnp.int32, links.shape[1:], 0)
+    mine = jnp.zeros(links.shape[1:], F32)
+    for s in range(1, seg_count):
+        parent = parents[s] - net.dp * seg_count
+        mine = jnp.where(half_at == s + 3, parent.astype(F32), mine)
+    links[0] = mine
+
     barrier = pltpu.get_barrier_semaphore()
     for device in greet:
         pl.semaphore_signal(barrier, inc=1, device_id=device, device_id_type=MESH)
@@ -682,12 +694,15 @@
             net.landed(dst.at[:, span(z, quarter)], first + 4 + z)
 
     vec_site = net.sites(3)
+    pltpu.make_async_copy(vec_in.at[pl.ds(0, 6), :], vec_in.at[pl.ds(0, 6), :], lsem.at[9]).wait()
     for o in (1, 2, 3):
-        net.send(vec_in, vec.at[:, span(row, quarter)], vec_site + o - 1, net.peer(dz=o))
+        net.send(
+            vec_in.at[pl.ds(0, 8), :], vec.at[:, span(row, quarter)], vec_site + o - 1, net.peer(dz=o)
+        )
+    links_site = net.sites(1)
+    net.send(links.at[0], links.at[1], links_site, net.rel(1))
     home_x, home_g = net.sites(8), net.sites(8)
     send_home(inp, lambda s: xs, home_x)
-    tab_site = net.sites(1)
-    net.send(tab, tab_far, tab_site, net.rel(1))
 
     def slices(w_ref, full, axis):
         if axis == 0:
@@ -709,17 +724,21 @@
 
         def start(self):
             own = pltpu.make_async_copy(
-                self.src_of(net.slice), self.place(row), lsem.at[self.local]
+                self.place(row), self.place(row), lsem.at[self.local]
             )
-            own.start()
+            for src, cols in self.src_of(net.slice):
+                pltpu.make_async_copy(
+                    src, self.place(row).at[:, cols], lsem.at[self.local]
+                ).start()
             for o in (1, 2, 3):
                 far = (zl ^ (o & 1)) * 2 + k
-                net.send(
-                    self.half(self.src_of(far), y),
-                    self.half(self.place(row), y),
-                    self.first + o - 1,
-                    net.peer(dz=o),
-                )
+                for src, cols in self.src_of(far):
+                    net.send(
+                        self.half(src, y),
+                        self.half(self.place(row), y).at[:, cols],
+                        self.first + o - 1,
+                        net.peer(dz=o),
+                    )
             self.own = own
 
         def relay(self):
@@ -734,9 +753,16 @@
             self.own.wait()
 
     hidden = hid.shape[1]
-    weight_q = Weight(lambda s: w_q.at[s], wq, 0, 0)
-    weight_d = Weight(lambda s: w_d.at[span(s, hidden), :], wd, 1, 2)
-    weight_u = Weight(lambda s: w_u.at[:, span(s, hidden)], wu, 0, 3)
+    whole = slice(None)
+
+    def qkv_parts(s):
+        return [
+            (w_q.at[n, :, span(s, head)], pl.ds(n * head, head)) for n in range(3)
+        ]
+
+    weight_q = Weight(qkv_parts, wq, 0, 0)
+    weight_d = Weight(lambda s: [(w_d.at[span(s, hidden), :], whole)], wd, 1, 2)
+    weight_u = Weight(lambda s: [(w_u.at[:, span(s, hidden)], whole)], wu, 0, 3)
     weight_q.start()
 
     gather_w = Gather(net, wf, shard // 2, over_y=True)
@@ -769,11 +795,21 @@
     weight_d.start()
     weight_q.relay()
 
-    net.landed(tab_far, tab_site)
-    table = jnp.where(zh == k, tab[...], tab_far[...])
+    net.landed(links.at[1], links_site)
+    parent = jnp.where(zh == k, links[0], links[1])[:, 0:1]
+    seg_len = tokens // 16
+    key_at = lax.broadcasted_iota(jnp.int32, (1, tokens), 1)
+    key_half = key_at // seg_len
+    key_seg = jnp.maximum(key_half - 3, 0)
+    half_row = lax.broadcasted_iota(jnp.int32, (16, 1), 0)
+    seg_row = jnp.maximum(half_row - 3, 0)
+    key_parent = jnp.sum(jnp.where(key_half == half_row, parent, 0.0), axis=0, keepdims=True)
+    start = jnp.where(key_parent > 0.0, 5 * seg_len, 4 * seg_len)
+    depth = jnp.where(key_seg == 0, key_at, start + key_at % seg_len)
+    allowed = (key_seg == 0) | (key_seg == seg_row) | (key_seg == parent.astype(jnp.int32))
     exponent = jnp.full((1, tokens), -(x * 4 + net.slice + 1), jnp.int32).astype(F32)
     slope = jnp.exp2(exponent)
-    bias[...] = jnp.where(table >= 0.0, slope * table, masked)
+    bias[...] = jnp.where(allowed, slope * depth.astype(F32), masked)
 
     b_q = b_qv[0:1, span(net.slice, head)]
     b_v = b_qv[1:2, span(net.slice, head)]
@@ -795,10 +831,6 @@
         v_buf[rows, :] = (proj[:, 2 * head :] + b_v).astype(BF)
 
     scale = head ** (-0.5)
-    seg_len = tokens // 16
-    key_at = lax.broadcasted_iota(jnp.int32, (1, tokens), 1)
-    key_half = key_at // seg_len
-    key_seg = jnp.maximum(key_half - 3, 0)
 
     def attend(i, carry):
         first = pl.multiple_of(i * shard, shard)
@@ -862,22 +894,11 @@
     gather_g.relay(2)
     gather_e2.relay(1)
     gather_e2.relay(2)
-    gather_g.relay(3)
-    weight_d.ready()
-    for j in range(4):
-        gather_g.ready(j)
-
-    def hidden_grad(c, carry):
-        rows = span(c, 2 * shard)
-        both = g[pl.ds(c * 2, 2)].reshape(2 * shard, width)
-        gh[rows, :] = dot_nt(both, wd[...])
-        return carry
-
-    lax.fori_loop(0, 4, hidden_grad, 0)
+
 
     b_u = b_up[0:1, span(net.slice, hidden)]
     weight_u.ready()
-    scatter_two = Scatter(net, part_set_a, landings(0))
+    scatter_two = Scatter(net, part_set_a, landings(0), shard // 2)
     for j in range(4):
         if j == 3:
             gather_e2.relay(3)
@@ -885,68 +906,89 @@
         pre = dot_nn(gather_e2.block(j), wu[...]) + b_u
         bell = 0.5 * (1.0 + lax.erf(pre * (1.0 / math.sqrt(2.0))))
         hid[rows_of(j), :] = (pre * bell).astype(BF)
+        if j == 0:
+            weight_d.ready()
+        if j == 3:
+            gather_g.relay(3)
+        gather_g.ready(j)
         rise = bell + pre * jnp.exp(-0.5 * pre * pre) * (1.0 / math.sqrt(2.0 * math.pi))
-        gp[rows_of(j), :] = (gh[rows_of(j), :] * rise).astype(BF)
+        gp[rows_of(j), :] = (dot_nt(gather_g.block(j), wd[...]) * rise).astype(BF)
         scatter_two.put(j, dot_nt(gp[rows_of(j), :], wu[...]))
         if j == 2:
             scatter_two.hop(1)
     scatter_two.hop(2)
     scatter_two.hop(3)
 
-    sum_d = TreeSum(net, dw_d, ly_d, yh_d, lz_d, fin_d, out_d, lsem.at[4])
-    sum_u = TreeSum(net, dw_u, ly_u, yh_u, lz_u, fin_u, out_u, lsem.at[5])
-    sum_o = TreeSum(net, dw_o, ly_o, yh_o, lz_o, fin_o, out_o, lsem.at[6])
-    sum_q = TreeSum(net, dw_q, ly_q, yh_q, lz_q, fin_q, out_q, lsem.at[7])
+    sums = {
+        name: TreeSum(net, own, land_y, hop, land_z, done, out, lsem.at[4 + n])
+        for n, (name, own, land_y, hop, land_z, done, out) in enumerate(
+            (
+                ("a", dw_a, ly_a, yh_a, lz_a, fin_a, out_a),
+                ("b", dw_b, ly_b, yh_b, lz_b, fin_b, out_b),
+                ("o", dw_o, ly_o, yh_o, lz_o, fin_o, out_o),
+                ("d", dw_d, ly_d, yh_d, lz_d, fin_d, out_d),
+                ("u", dw_u, ly_u, yh_u, lz_u, fin_u, out_u),
+            )
+        )
+    }
 
     def columns(buf, z):
         part = buf[:, :, span(z, quarter)]
         return part.reshape(tokens, quarter)
 
     def grad_down(z, carry):
-        sum_d.put(z, dot_tn(hid[...], columns(g, z)))
+        sums["d"].put(z, dot_tn(hid[...], columns(g, z)))
         return carry
 
+    def grad_up(z, carry):
+        sums["u"].put(z, dot_tn(columns(e2, z), gp[...]))
+        return carry
+
+    def grad_qkv(z, carry):
+        value = dot_tn(columns(e1, z), dqkv[...])
+        sums["a"].put(z, value[:, :head])
+        sums["b"].put(z, value[:, head:])
+        return carry
+
+    def grad_o(z, carry):
+        sums["o"].put(z, dot_tn(mix_b[...], columns(gb, z)))
+        return carry
+
     lax.fori_loop(0, 4, grad_down, 0)
-    sum_d.start()
+    sums["d"].start()
     scatter_two.hop_on()
-
-    def grad_up(z, carry):
-        sum_u.put(z, dot_tn(columns(e2, z), gp[...]))
-        return carry
-
     lax.fori_loop(0, 4, grad_up, 0)
-    sum_u.start()
 
     grad = scatter_two.total()
     middle = mid[...]
     normed, inv = norm_stats(middle)
-    tok[2:3, :] = jnp.sum(grad * normed, axis=0, keepdims=True)
-    tok[3:4, :] = jnp.sum(grad, axis=0, keepdims=True)
     spread = grad * vec[3:4, :]
     mean_one = jnp.sum(spread, axis=1, keepdims=True) * (1.0 / width)
     mean_two = jnp.sum(spread * normed, axis=1, keepdims=True) * (1.0 / width)
     cot_own = g[net.slot].astype(F32)
-    tok[5:6, :] = jnp.sum(cot_own, axis=0, keepdims=True)
     total = cot_own + inv * (spread - mean_one - normed * mean_two)
     gmid[...] = total
     branch = total.astype(BF)
     gb[net.slot] = branch
-    tok[4:5, :] = jnp.sum(branch.astype(F32), axis=0, keepdims=True)
-    tok[6:8, :] = jnp.zeros((2, width), F32)
     grad_all[...] = dot_nt(branch, w_out).astype(BF)
     swap_back = Exchange(
         net, lambda h: grad_all.at[:, span(h, head)], lambda q: gm.at[span(q, shard), :]
     )
     swap_back.start()
     gm[span(net.slot, shard), :] = grad_all[:, span(net.slot, head)]
-    gather_gb = Gather(net, gb, shard // 2)
-    gather_gb.start()
-
+    tok[2:3, :] = jnp.sum(grad * normed, axis=0, keepdims=True)
+    tok[3:4, :] = jnp.sum(grad, axis=0, keepdims=True)
+    tok[4:5, :] = jnp.sum(branch.astype(F32), axis=0, keepdims=True)
+    tok[5:6, :] = jnp.sum(cot_own, axis=0, keepdims=True)
+    tok[6:8, :] = jnp.zeros((2, width), F32)
     dk_acc[...] = jnp.zeros_like(dk_acc)
     dv_acc[...] = jnp.zeros_like(dv_acc)
-
-    def attend_back(first):
-        rows = pl.ds(first, shard)
+    small[...] = jnp.zeros_like(small)
+    small[0:1, :] = jnp.sum(gp[...].astype(F32), axis=0, keepdims=True)
+    gather_gb = Gather(net, gb, 0)
+
+    def tile_back(t, carry):
+        rows = span(t, shard)
         grad_mix = gm[rows, :]
         probs = p_buf[rows, :]
         grad_probs = dot_nt(grad_mix, v_buf[...])
@@ -955,45 +997,41 @@
         dqkv[rows, :head] = (dot_nn(grad_scores, k_buf[...]) * scale).astype(BF)
         dk_acc[...] += dot_tn(grad_scores, q_buf[rows, :])
         dv_acc[...] += dot_tn(probs, grad_mix)
+        return carry
 
     swap_back.ready()
-
-    def tile_back(t, carry):
-        attend_back(pl.multiple_of(t * shard, shard))
-        return carry
-
-    lax.fori_loop(0, 5, tile_back, 0)
+    gather_gb.start()
+    sums["d"].across()
+    sums["u"].start()
+    lax.fori_loop(0, 8, tile_back, 0)
+    dqkv[:, head : 2 * head] = (dk_acc[...] * scale).astype(BF)
+    dqkv[:, 2 * head :] = dv_acc[...].astype(BF)
     gather_gb.relay(1)
     gather_gb.relay(2)
-    lax.fori_loop(5, 8, tile_back, 0)
-    dqkv[:, head : 2 * head] = (dk_acc[...] * scale).astype(BF)
-    dqkv[:, 2 * head :] = dv_acc[...].astype(BF)
-
-    scatter_four = Scatter(net, part_set_a, landings(1))
+
+    scatter_four = Scatter(net, part_set_a, landings(1), shard // 2)
     scatter_two.left()
     for j in order:
         scatter_four.put(j, dot_nt(dqkv[rows_of(j), :], wq[...]))
     for j in (3, 1, 2):
         scatter_four.hop(j)
-    sum_d.across()
-
-    def grad_qkv(z, carry):
-        sum_q.put(z, dot_tn(columns(e1, z), dqkv[...]))
-        return carry
-
     lax.fori_loop(0, 4, grad_qkv, 0)
-    sum_q.start()
     scatter_four.hop_on()
-    sum_u.across()
-
-    small[...] = jnp.zeros_like(small)
-    small[0:1, :] = jnp.sum(gp[...].astype(F32), axis=0, keepdims=True)
+    sums["u"].across()
+    sums["b"].start()
+    sums["a"].start()
+    sums["d"].hand_out()
+
     small[1:2, :head] = jnp.sum(dqkv[:, :head].astype(F32), axis=0, keepdims=True)
     small[1:2, head : 2 * head] = jnp.sum(dqkv[:, 2 * head :].astype(F32), axis=0, keepdims=True)
     small_site = net.sites(6)
     others = ((1, 0), (0, 2), (1, 2))
     for n, (dy, dz) in enumerate(others):
         net.send(small, small_land.at[n], small_site + n, net.peer(dy=dy, dz=dz))
+    gather_gb.relay(3)
+    for j in range(4):
+        gather_gb.ready(j)
+    lax.fori_loop(0, 4, grad_o, 0)
 
     def send_out(src, dst, first):
         for z in range(4):
@@ -1024,30 +1062,28 @@
     back_b[...] = (gmid[...] + inv * (spread - mean_one - normed * mean_two)).astype(BF)
     send_out(back_b, grad_out, grad_site)
 
-    sum_d.hand_out()
-    sum_q.across()
-    gather_gb.relay(3)
-    for j in range(4):
-        gather_gb.ready(j)
-
-    def grad_o(z, carry):
-        sum_o.put(z, dot_tn(mix_b[...], columns(gb, z)))
-        return carry
-
-    lax.fori_loop(0, 4, grad_o, 0)
-    sum_o.start()
-    scatter_three = Scatter(net, part_set_b, landings(2))
+    scatter_three = Scatter(net, part_set_b, landings(2), shard)
     for j in order:
         scatter_three.put(j, dot_nn(hid[rows_of(j), :], wd[...]))
     for j in (3, 1, 2):
         scatter_three.hop(j)
-    sum_u.hand_out()
-    sum_d.pass_on()
-    sum_o.across()
+    sums["d"].pass_on()
+    sums["b"].across()
+    sums["a"].across()
+    sums["o"].start()
+    sums["u"].hand_out()
     scatter_three.hop_on()
-    sum_q.hand_out()
-    sum_u.pass_on()
-    sum_d.share()
+    sums["o"].across()
+    sums["b"].hand_out()
+    sums["a"].hand_out()
+    sums["u"].pass_on()
+    sums["d"].share()
+    back_a[...] = (mid[...] + scatter_three.total() + vec[5:6, :]).astype(BF)
+    send_out(back_a, res_out, res_site)
+    sums["b"].pass_on()
+    sums["a"].pass_on()
+    sums["o"].hand_out()
+    sums["u"].share()
     acc = small[...]
     for n in range(3):
         net.landed(small_land.at[n], small_site + n)
@@ -1063,28 +1099,31 @@
         net.landed(tok_one.at[n], tok_site + n)
         acc = acc + tok_one[n]
     tok_sum[...] = acc
-    for n, (dy, dz) in enumerate(others):
+    tok_sent = [
         net.send(tok_sum, tok_two.at[n], tok_site + 7 + n, net.peer(dy=dy, dz=dz))
-    sum_o.hand_out()
-    sum_q.pass_on()
-    sum_u.share()
-    sum_o.pass_on()
-    back_a[...] = (mid[...] + scatter_three.total() + vec[5:6, :]).astype(BF)
-    send_out(back_a, res_out, res_site)
-    sum_q.share()
-    sum_o.share()
+        for n, (dy, dz) in enumerate(others)
+    ]
+    gone = {id(remote) for remote in tok_sent}
+    net.pending = [p for p in net.pending if id(p[0]) not in gone]
+    sums["o"].pass_on()
+    sums["b"].share()
+    sums["a"].share()
+    sums["o"].share()
     for n in range(3):
         net.landed(tok_two.at[n], tok_site + 7 + n)
         acc = acc + tok_two[n]
-    out_tok[...] = acc
+    for remote in tok_sent:
+        remote.wait_send()
+    tok_sum[...] = acc
+    out_tok[...] = tok_sum[:, span(row, quarter)]
     for n, flip in enumerate((1, 2, 3)):
         net.landed(out_small.at[net.slice ^ flip], small_site + 3 + n)
-    for one_sum in (sum_d, sum_u, sum_q, sum_o):
+    for one_sum in sums.values():
         one_sum.finish()
     out_ready(res_out, res_site)
     out_ready(grad_out, grad_site)
     net.drain()
-    sems.append(net.used)
+    used.append(net.used)
 
 
 def layer_on_square(
@@ -1099,22 +1138,6 @@
     hidden = w_up.shape[1] // slices
     row = lax.axis_index("row")
 
-    seg_len = tokens // 16
-    parent = seg_parent - lax.axis_index("dp") * seg_parent.shape[0]
-    seg = jnp.maximum(jnp.arange(16, dtype=jnp.int32) - 3, 0)
-    key_seg = jnp.repeat(seg, seg_len)
-    ids = jnp.arange(seg_parent.shape[0], dtype=jnp.int32)
-    up_one = jnp.sum(jnp.where(seg[:, None] == ids[None, :], parent[None, :], 0), axis=1)
-    up_two = jnp.sum(jnp.where(up_one[:, None] == ids[None, :], parent[None, :], 0), axis=1)
-    keys = key_seg[None, :]
-    allowed = (keys == seg[:, None]) | (keys == up_one[:, None]) | (keys == up_two[:, None])
-    table = jnp.where(allowed, token_depth[None, :].astype(F32), -1.0)
-
-    w_q = w_qkv.reshape(quarter, 3, slices, head).transpose(2, 0, 1, 3)
-    w_q = w_q.reshape(slices, quarter, 3 * head)
-    blank = jnp.zeros_like(ln1_gain)
-    vectors = jnp.stack([ln1_gain, ln1_bias, b_out, ln2_gain, ln2_bias, b_down, blank, blank])
-
     any_ = pl.BlockSpec(memory_space=pl.ANY)
     vmem = pl.BlockSpec(memory_space=pltpu.VMEM)
     sds = jax.ShapeDtypeStruct
@@ -1122,27 +1145,31 @@
     def vm(*dims, dtype=BF):
         return pltpu.VMEM(dims, dtype)
 
-    blocks = {"q": (quarter, 3 * head), "o": (head, quarter), "d": (hidden, quarter), "u": (quarter, hidden)}
-    names = ("q", "o", "d", "u")
+    blocks = {
+        "a": (quarter, head), "b": (quarter, 2 * head), "o": (head, quarter),
+        "d": (hidden, quarter), "u": (quarter, hidden),
+    }
+    names = ("a", "b", "o", "d", "u")
     halves = {n: (blocks[n][0] // 2, blocks[n][1]) for n in names}
     scratch = [
         vm(shard, width),
         *[vm(8, shard, width) for _ in range(5)],
         vm(width, 3 * head), vm(hidden, width), vm(width, hidden),
         vm(shard, width), vm(shard, width),
-        vm(16, tokens, dtype=F32), vm(8, width, dtype=F32), vm(16, tokens, dtype=F32),
+        vm(2, 16, 128, dtype=F32), vm(8, quarter, dtype=F32), vm(8, width, dtype=F32),
+        vm(16, tokens, dtype=F32),
         *[vm(tokens, head) for _ in range(3)], vm(tokens, tokens),
         vm(tokens, head, dtype=F32), vm(tokens, head),
         *[
             spec
             for _ in range(2)
             for spec in (
-                vm(8, shard, width), vm(4, shard // 2, width),
-                vm(2, shard // 2, width, dtype=F32), vm(2, shard // 2, width),
+                vm(8, shard, width), vm(2, shard, width),
+                vm(shard, width, dtype=F32), vm(shard, width),
             )
         ],
-        vm(3, 4, shard, width), vm(3, 4, shard // 2, width), vm(3, 2, shard // 2, width),
-        vm(tokens, hidden, dtype=F32), vm(tokens, hidden), vm(tokens, hidden),
+        vm(3, 4, shard, width), vm(3, 2, shard, width), vm(3, shard, width),
+        vm(tokens, hidden), vm(tokens, hidden),
         vm(tokens, head), vm(tokens, head, dtype=F32), vm(tokens, head, dtype=F32),
         vm(tokens, 3 * head),
         vm(shard, width, dtype=F32), vm(shard, width, dtype=F32), vm(shard, width), vm(shard, width),
@@ -1154,8 +1181,8 @@
         vm(8, width, dtype=F32), vm(7, 8, width, dtype=F32), vm(8, width, dtype=F32),
         vm(3, 8, width, dtype=F32),
         vm(8, hidden, dtype=F32), vm(3, 8, hidden, dtype=F32), vm(8, hidden, dtype=F32),
-        pltpu.SemaphoreType.DMA((200,)), pltpu.SemaphoreType.DMA((200,)),
-        pltpu.SemaphoreType.DMA((8,)),
+        pltpu.SemaphoreType.DMA((208,)), pltpu.SemaphoreType.DMA((208,)),
+        pltpu.SemaphoreType.DMA((10,)),
     ]
     used = []
     outs = pl.pallas_call(
@@ -1163,44 +1190,82 @@
         out_shape=(
             sds((half_tokens, quarter), BF), sds((half_tokens, quarter), BF),
             *[sds((slices, *blocks[n]), BF) for n in names],
-            sds((8, width), F32), sds((slices, 8, hidden), F32),
+            sds((8, quarter), F32), sds((slices, 8, hidden), F32),
         ),
-        in_specs=[any_] * 6 + [vmem] * 4,
-        out_specs=(any_,) * 6 + (vmem,) * 2,
+        in_specs=[any_] * 12 + [pl.BlockSpec(memory_space=pltpu.SMEM)] + [vmem] * 2,
+        out_specs=(any_,) * 7 + (vmem,) * 2,
         scratch_shapes=scratch,
         compiler_params=pltpu.CompilerParams(
             collective_id=0, has_side_effects=True, vmem_limit_bytes=60 << 20
         ),
         name="tree_layer",
     )(
-        inputs, cotangent, w_q, w_out, w_down, w_up, table, vectors,
-        b_up.reshape(1, -1), b_qv,
-    )
-    result, input_grad, g_q, g_o, g_u, g_d, by_token, small = (
-        outs[0], outs[1], outs[2], outs[3], outs[5], outs[4], outs[6], outs[7],
-    )
-    by_token = lax.dynamic_slice_in_dim(by_token, row * quarter, quarter, 1)
-    grad_w_qkv = g_q.reshape(slices, quarter, 3, head).transpose(1, 2, 0, 3)
-    grad_w_qkv = grad_w_qkv.reshape(quarter, 3, slices * head).astype(F32)
-    grad_w_up = g_u.transpose(1, 0, 2).reshape(quarter, slices * hidden).astype(F32)
-    grad_b_qv = jnp.stack(
-        [small[:, 1, :head].reshape(-1), small[:, 1, head : 2 * head].reshape(-1)]
-    )
+        inputs, cotangent, w_qkv.transpose(1, 0, 2), w_out, w_down, w_up,
+        *[v.reshape(1, -1) for v in (ln1_gain, ln1_bias, b_out, ln2_gain, ln2_bias, b_down)],
+        seg_parent, b_up.reshape(1, -1), b_qv,
+    )
+    result, input_grad, g_a, g_b, g_o, g_d, g_u, by_token, small = outs
+    steps = 2
+
+    def finish(res_in, grad_in, a_in, b_in, o_in, d_in, u_in, tok_in, small_in, *into):
+        res, grad, q, o, d, u, tok_0, tok_1, tok_2, tok_3, tok_4, tok_5, up, qv = into
+        res[...] = res_in[...].astype(F32)
+        grad[...] = grad_in[...].astype(F32)
+        o[...] = o_in[...].astype(F32)
+        d[...] = d_in[...].astype(F32)
+        for s in range(slices):
+            u[:, s * hidden : (s + 1) * hidden] = u_in[s].astype(F32)
+            at = slice(s * head, (s + 1) * head)
+            q[0, :, at] = a_in[s].astype(F32)
+            for n in range(2):
+                q[n + 1, :, at] = b_in[s, :, n * head : (n + 1) * head].astype(F32)
+            up[0:1, s * hidden : (s + 1) * hidden] = small_in[s, 0:1, :]
+            for n in range(2):
+                qv[n : n + 1, at] = small_in[
+                    s, 1:2, n * head : (n + 1) * head
+                ]
+        for n, one in enumerate((tok_0, tok_1, tok_2, tok_3, tok_4, tok_5)):
+            one[...] = tok_in[n : n + 1, :]
+
+    def rows(*dims):
+        return pl.BlockSpec((dims[0] // steps, *dims[1:]), lambda i: (i,) + (0,) * (len(dims) - 1))
+
+    def middle(*dims):
+        return pl.BlockSpec((dims[0], dims[1] // steps, *dims[2:]), lambda i: (0, i, 0))
+
+    def fixed(*dims):
+        return pl.BlockSpec(dims, lambda i: (0,) * len(dims))
+
+    tall_o, tall_d = (slices * head, quarter), (slices * hidden, quarter)
+    done = pl.pallas_call(
+        finish,
+        grid=(steps,),
+        out_shape=(
+            sds((half_tokens, quarter), F32), sds((half_tokens, quarter), F32),
+            sds((3, quarter, slices * head), F32), sds(tall_o, F32), sds(tall_d, F32),
+            sds((quarter, slices * hidden), F32), *[sds((1, quarter), F32)] * 6,
+            sds((1, slices * hidden), F32), sds((2, slices * head), F32),
+        ),
+        in_specs=[
+            rows(half_tokens, quarter), rows(half_tokens, quarter),
+            middle(slices, *blocks["a"]), middle(slices, *blocks["b"]), rows(*tall_o), rows(*tall_d), middle(slices, *blocks["u"]),
+            fixed(8, quarter), fixed(slices, 8, hidden),
+        ],
+        out_specs=(
+            rows(half_tokens, quarter), rows(half_tokens, quarter),
+            middle(3, quarter, slices * head), rows(*tall_o), rows(*tall_d),
+            rows(quarter, slices * hidden), *[fixed(1, quarter)] * 6,
+            fixed(1, slices * hidden), fixed(2, slices * head),
+        ),
+        compiler_params=pltpu.CompilerParams(vmem_limit_bytes=60 << 20),
+        name="finish",
+    )(
+        result, input_grad, g_a, g_b, g_o.reshape(tall_o), g_d.reshape(tall_d), g_u, by_token, small
+    )
+    by_token = [v.reshape(-1) for v in done[6:12]]
     return (
-        result.astype(F32),
-        input_grad.astype(F32),
-        by_token[0],
-        by_token[1],
-        grad_w_qkv,
-        grad_b_qv,
-        g_o.reshape(slices * head, quarter).astype(F32),
-        by_token[4],
-        by_token[2],
-        by_token[3],
-        grad_w_up,
-        small[:, 0].reshape(-1),
-        g_d.reshape(slices * hidden, quarter).astype(F32),
-        by_token[5],
+        done[0], done[1], by_token[0], by_token[1], done[2].transpose(1, 0, 2), done[13], done[3], by_token[4],
+        by_token[2], by_token[3], done[5], done[12].reshape(-1), done[4], by_token[5],
     )
 
 

time: 197 us -> 177 us (0.90); the launches traced: 197 us -> 175 us
  local copies, waits for them, and re-layouts: 14 us -> 0 us
  other arithmetic: 8.59 us -> 0 us
    convert_element_type x6 -> x0, other arithmetic: 6.24 us -> none  [the longest x1 1.55 us: layer_on_square(): g_d.reshape(slices * hidden, quarter).astype(F32)]
    unnamed x25 -> x0, local copies, waits for them, and re-layouts: 6.08 us -> none
    pallas_call x0 -> x1, Pallas kernels: none -> 4.74 us  [layer_on_square(): pl.pallas_call(finish, grid=(steps,), out_shape=(sds((half_tokens, quarte...]
    pallas_call x1, Pallas kernels: 174 us -> 169 us  [layer_on_square(): pl.pallas_call(functools.partial(layer_kernel, EPS, MASKED, used), out_sh...]
    slice x2 -> x0, local copies, waits for them, and re-layouts: 3.01 us -> none  [the longest x1 1.57 us: layer_on_square(): by_token[5]]
    convert_element_type x3 -> x0, local copies, waits for them, and re-layouts: 2.2 us -> none  [the longest x1 1.81 us: layer_on_square(): g_u.transpose(1, 0, 2).reshape(quarter, slices * hidden).astype(F32)]
where the time goes in v3:
time: 177 us; the launch traced here: 175 us
  Pallas kernels  174 us (98%)
    pallas_call x1, Pallas kernels, layer_on_square(): pl.pallas_call(functools.partial(layer_kernel, EPS, MASKED, used), out_sh...  169 us
    pallas_call x1, Pallas kernels, layer_on_square(): pl.pallas_call(finish, grid=(steps,), out_shape=(sds((half_tokens, quarte...  4.74 us

profile of v3, /device:TPU:0, one launch (start us, length us, event | category | flops | bytes accessed | tf_op | source)
XLA Modules:
  0.0 174.9 jit_solution(11441997086352401417)
XLA Ops:
  0.7 169.3 %tree_layer.1 = (bf16[512,256]{1,0:T(8,128)(2,1)}, bf16[512,256]{1,0:T(8,128)(2,1)}, bf16[4,256,128]{2,1,0:T(8,128)(2,1)}, bf16[4,256,256]{2,1,0:T(8,128)(2,1)},...) custom-call(bf16[512,256]{1,0:T(8,128)(2,1)} %refs_0_.1, ...), custom_call_target="tpu_custom_call" | custom-call | tf_op jit(solution)/shard_map/tree_layer/pallas_call | solution.py:1188
  170.0 4.7 %finish.1 = (f32[512,256]{1,0:T(8,128)}, f32[512,256]{1,0:T(8,128)}, f32[3,256,512]{2,1,0:T(8,128)}, f32[512,256]{1,0:T(8,128)}, f32[2048,256]{1,0:T(8,128)}, /*...) custom-call(bf16[512,256]{1,0:T(8,128)(2,1)} %get-tuple-element.37.r, ...), custom_call_target="tpu_custom_call" | custom-call | tf_op jit(solution)/shard_map/finish/pallas_call | solution.py:1240

commit v4 on v3

--- a/solution.py
+++ b/solution.py
@@ -569,11 +569,11 @@
 
 
 class TreeSum:
-    def __init__(self, net, own, land_y, hop, land_z, done, out, local_sem):
+    def __init__(self, net, own, land_y, hop, land_z, done, out, local_sem, direct):
         self.net, self.own, self.land_y = net, own, land_y
         self.hop_buf, self.land_z, self.done, self.out = hop, land_z, done, out
         self.first = net.sites(7)
-        self.local_sem = local_sem
+        self.local_sem, self.direct = local_sem, direct
 
     def put(self, z, value):
         rows = self.own.shape[3]
@@ -608,6 +608,8 @@
         place = self.half(net.slice, net.y)
         net.send(self.done.at[1 - net.zl], place, self.first + 2, net.peer(dz=1))
         net.send(self.done.at[net.zl], place, self.first + 3, net.peer(dy=1))
+        if self.direct:
+            net.send(self.done.at[1 - net.zl], place, self.first + 4, net.peer(dy=1, dz=1))
         self.kept = pltpu.make_async_copy(self.done.at[net.zl], place, self.local_sem)
         self.kept.start()
 
@@ -615,7 +617,8 @@
         net = self.net
         part = self.half(net.slice ^ 2, net.y)
         net.landed(part, self.first + 2)
-        net.send(part, part, self.first + 4, net.peer(dy=1))
+        if not self.direct:
+            net.send(part, part, self.first + 4, net.peer(dy=1))
 
     def share(self):
         net = self.net
@@ -660,6 +663,9 @@
         if dy + dk + dz
     ]
     greet += [net.peer(dk=dk, dz=dz, dx=1) for dk in (0, 1) for dz in (0, 1)]
+    barrier = pltpu.get_barrier_semaphore()
+    for device in greet:
+        pl.semaphore_signal(barrier, inc=1, device_id=device, device_id_type=MESH)
     vec_parts = (vec_0, vec_1, vec_2, vec_3, vec_4, vec_5)
     for n, part in enumerate(vec_parts):
         pltpu.make_async_copy(part, vec_in.at[pl.ds(n, 1), :], lsem.at[9]).start()
@@ -671,9 +677,6 @@
         mine = jnp.where(half_at == s + 3, parent.astype(F32), mine)
     links[0] = mine
 
-    barrier = pltpu.get_barrier_semaphore()
-    for device in greet:
-        pl.semaphore_signal(barrier, inc=1, device_id=device, device_id_type=MESH)
     pl.semaphore_wait(barrier, len(greet))
 
     def send_home(src, dst_of, first):
@@ -791,8 +794,6 @@
     gather_e1.start()
     gather_g = Gather(net, g, 0)
     send_home(cot, lambda s: g.at[x * 4 + s], home_g)
-    weight_u.start()
-    weight_d.start()
     weight_q.relay()
 
     net.landed(links.at[1], links_site)
@@ -815,6 +816,8 @@
     b_v = b_qv[1:2, span(net.slice, head)]
     gather_e1.relay(1)
     gather_e1.relay(2)
+    weight_u.start()
+    weight_d.start()
     weight_q.ready()
     for j in range(4):
         if j == 3:
@@ -920,7 +923,7 @@
     scatter_two.hop(3)
 
     sums = {
-        name: TreeSum(net, own, land_y, hop, land_z, done, out, lsem.at[4 + n])
+        name: TreeSum(net, own, land_y, hop, land_z, done, out, lsem.at[4 + n], name in "o")
         for n, (name, own, land_y, hop, land_z, done, out) in enumerate(
             (
                 ("a", dw_a, ly_a, yh_a, lz_a, fin_a, out_a),
@@ -958,6 +961,7 @@
     sums["d"].start()
     scatter_two.hop_on()
     lax.fori_loop(0, 4, grad_up, 0)
+    sums["u"].start()
 
     grad = scatter_two.total()
     middle = mid[...]
@@ -1001,13 +1005,9 @@
 
     swap_back.ready()
     gather_gb.start()
-    sums["d"].across()
-    sums["u"].start()
     lax.fori_loop(0, 8, tile_back, 0)
     dqkv[:, head : 2 * head] = (dk_acc[...] * scale).astype(BF)
     dqkv[:, 2 * head :] = dv_acc[...].astype(BF)
-    gather_gb.relay(1)
-    gather_gb.relay(2)
 
     scatter_four = Scatter(net, part_set_a, landings(1), shard // 2)
     scatter_two.left()
@@ -1015,6 +1015,9 @@
         scatter_four.put(j, dot_nt(dqkv[rows_of(j), :], wq[...]))
     for j in (3, 1, 2):
         scatter_four.hop(j)
+    sums["d"].across()
+    gather_gb.relay(1)
+    gather_gb.relay(2)
     lax.fori_loop(0, 4, grad_qkv, 0)
     scatter_four.hop_on()
     sums["u"].across()
@@ -1032,6 +1035,7 @@
     for j in range(4):
         gather_gb.ready(j)
     lax.fori_loop(0, 4, grad_o, 0)
+    sums["o"].start()
 
     def send_out(src, dst, first):
         for z in range(4):
@@ -1070,7 +1074,6 @@
     sums["d"].pass_on()
     sums["b"].across()
     sums["a"].across()
-    sums["o"].start()
     sums["u"].hand_out()
     scatter_three.hop_on()
     sums["o"].across()
@@ -1078,11 +1081,11 @@
     sums["a"].hand_out()
     sums["u"].pass_on()
     sums["d"].share()
+    sums["o"].hand_out()
     back_a[...] = (mid[...] + scatter_three.total() + vec[5:6, :]).astype(BF)
     send_out(back_a, res_out, res_site)
     sums["b"].pass_on()
     sums["a"].pass_on()
-    sums["o"].hand_out()
     sums["u"].share()
     acc = small[...]
     for n in range(3):
@@ -1105,9 +1108,9 @@
     ]
     gone = {id(remote) for remote in tok_sent}
     net.pending = [p for p in net.pending if id(p[0]) not in gone]
-    sums["o"].pass_on()
     sums["b"].share()
     sums["a"].share()
+    sums["o"].pass_on()
     sums["o"].share()
     for n in range(3):
         net.landed(tok_two.at[n], tok_site + 7 + n)

time: 177 us -> 169 us (0.955); the launches traced: 175 us -> 169 us
  Pallas kernels: 174 us -> 168 us
    pallas_call x1, Pallas kernels: 169 us -> 164 us  [layer_on_square(): pl.pallas_call(functools.partial(layer_kernel, EPS, MASKED, used), out_sh...]
where the time goes in v4:
time: 169 us
  Pallas kernels  168 us (99%)
    pallas_call x1, Pallas kernels, layer_on_square(): pl.pallas_call(functools.partial(layer_kernel, EPS, MASKED, used), out_sh...  164 us
    pallas_call x1, Pallas kernels, layer_on_square(): pl.pallas_call(finish, grid=(steps,), out_shape=(sds((half_tokens, quarte...  4.74 us

profile of v4, /device:TPU:0, one launch (start us, length us, event | category | flops | bytes accessed | tf_op | source)
XLA Modules:
  0.0 169.1 jit_solution(349357035306774278)
XLA Ops:
  0.7 163.6 %tree_layer.1 = (bf16[512,256]{1,0:T(8,128)(2,1)}, bf16[512,256]{1,0:T(8,128)(2,1)}, bf16[4,256,128]{2,1,0:T(8,128)(2,1)}, bf16[4,256,256]{2,1,0:T(8,128)(2,1)},...) custom-call(bf16[512,256]{1,0:T(8,128)(2,1)} %refs_0_.1, ...), custom_call_target="tpu_custom_call" | custom-call | tf_op jit(solution)/shard_map/tree_layer/pallas_call | solution.py:1191
  164.2 4.7 %finish.1 = (f32[512,256]{1,0:T(8,128)}, f32[512,256]{1,0:T(8,128)}, f32[3,256,512]{2,1,0:T(8,128)}, f32[512,256]{1,0:T(8,128)}, f32[2048,256]{1,0:T(8,128)}, /*...) custom-call(bf16[512,256]{1,0:T(8,128)(2,1)} %get-tuple-element.37.r, ...), custom_call_target="tpu_custom_call" | custom-call | tf_op jit(solution)/shard_map/finish/pallas_call | solution.py:1243

commit v5 on v4

--- a/solution.py
+++ b/solution.py
@@ -766,16 +766,11 @@
     weight_q = Weight(qkv_parts, wq, 0, 0)
     weight_d = Weight(lambda s: [(w_d.at[span(s, hidden), :], whole)], wd, 1, 2)
     weight_u = Weight(lambda s: [(w_u.at[:, span(s, hidden)], whole)], wu, 0, 3)
-    weight_q.start()
 
     gather_w = Gather(net, wf, shard // 2, over_y=True)
     wf_own = wf.at[gather_w.slot]
     wf_site = net.sites(3)
     wf_src = w_o.at[span(y * 2 + k, shard), :]
-    wf_copy = pltpu.make_async_copy(wf_src, wf_own.at[:, span(row, quarter)], lsem.at[1])
-    wf_copy.start()
-    for o in (1, 2, 3):
-        net.send(wf_src, wf_own.at[:, span(row, quarter)], wf_site + o - 1, net.peer(dz=o))
 
     vec[:, span(row, quarter)] = vec_in[...]
     for o in (1, 2, 3):
@@ -787,11 +782,16 @@
         inv = lax.rsqrt(msq - mean * mean + eps)
         return (values - mean) * inv, inv
 
+    weight_q.start()
     home_ready(xs, home_x)
     normed, _ = norm_stats(xs[...].astype(F32))
     e1[net.slot] = (normed * vec[0:1, :] + vec[1:2, :]).astype(BF)
     gather_e1 = Gather(net, e1, 0)
     gather_e1.start()
+    wf_copy = pltpu.make_async_copy(wf_src, wf_own.at[:, span(row, quarter)], lsem.at[1])
+    wf_copy.start()
+    for o in (1, 2, 3):
+        net.send(wf_src, wf_own.at[:, span(row, quarter)], wf_site + o - 1, net.peer(dz=o))
     gather_g = Gather(net, g, 0)
     send_home(cot, lambda s: g.at[x * 4 + s], home_g)
     weight_q.relay()
@@ -1082,21 +1082,6 @@
     sums["u"].pass_on()
     sums["d"].share()
     sums["o"].hand_out()
-    back_a[...] = (mid[...] + scatter_three.total() + vec[5:6, :]).astype(BF)
-    send_out(back_a, res_out, res_site)
-    sums["b"].pass_on()
-    sums["a"].pass_on()
-    sums["u"].share()
-    acc = small[...]
-    for n in range(3):
-        net.landed(small_land.at[n], small_site + n)
-        acc = acc + small_land[n]
-    small_sum[...] = acc
-    out_small[net.slice] = acc
-    for n, (dk, dz) in enumerate(((1, 0), (0, 1), (1, 1))):
-        net.send(
-            small_sum, out_small.at[net.slice], small_site + 3 + n, net.peer(dk=dk, dz=dz)
-        )
     acc = tok[...]
     for n in range(7):
         net.landed(tok_one.at[n], tok_site + n)
@@ -1108,6 +1093,21 @@
     ]
     gone = {id(remote) for remote in tok_sent}
     net.pending = [p for p in net.pending if id(p[0]) not in gone]
+    back_a[...] = (mid[...] + scatter_three.total() + vec[5:6, :]).astype(BF)
+    send_out(back_a, res_out, res_site)
+    sums["b"].pass_on()
+    sums["a"].pass_on()
+    sums["u"].share()
+    acc_s = small[...]
+    for n in range(3):
+        net.landed(small_land.at[n], small_site + n)
+        acc_s = acc_s + small_land[n]
+    small_sum[...] = acc_s
+    out_small[net.slice] = acc_s
+    for n, (dk, dz) in enumerate(((1, 0), (0, 1), (1, 1))):
+        net.send(
+            small_sum, out_small.at[net.slice], small_site + 3 + n, net.peer(dk=dk, dz=dz)
+        )
     sums["b"].share()
     sums["a"].share()
     sums["o"].pass_on()

time: 169 us -> 167 us (0.988)
  Pallas kernels: 168 us -> 166 us
    pallas_call x1, Pallas kernels: 164 us -> 162 us  [layer_on_square(): pl.pallas_call(functools.partial(layer_kernel, EPS, MASKED, used), out_sh...]
where the time goes in v5:
time: 167 us
  Pallas kernels  166 us (99%)
    pallas_call x1, Pallas kernels, layer_on_square(): pl.pallas_call(functools.partial(layer_kernel, EPS, MASKED, used), out_sh...  162 us
    pallas_call x1, Pallas kernels, layer_on_square(): pl.pallas_call(finish, grid=(steps,), out_shape=(sds((half_tokens, quarte...  4.74 us

profile of v5, /device:TPU:0, one launch (start us, length us, event | category | flops | bytes accessed | tf_op | source)
XLA Modules:
  0.0 167.3 jit_solution(17523299548587456911)
XLA Ops:
  0.7 161.7 %tree_layer.1 = (bf16[512,256]{1,0:T(8,128)(2,1)}, bf16[512,256]{1,0:T(8,128)(2,1)}, bf16[4,256,128]{2,1,0:T(8,128)(2,1)}, bf16[4,256,256]{2,1,0:T(8,128)(2,1)},...) custom-call(bf16[512,256]{1,0:T(8,128)(2,1)} %refs_0_.1, ...), custom_call_target="tpu_custom_call" | custom-call | tf_op jit(solution)/shard_map/tree_layer/pallas_call | solution.py:1191
  162.4 4.7 %finish.1 = (f32[512,256]{1,0:T(8,128)}, f32[512,256]{1,0:T(8,128)}, f32[3,256,512]{2,1,0:T(8,128)}, f32[512,256]{1,0:T(8,128)}, f32[2048,256]{1,0:T(8,128)}, /*...) custom-call(bf16[512,256]{1,0:T(8,128)(2,1)} %get-tuple-element.37.r, ...), custom_call_target="tpu_custom_call" | custom-call | tf_op jit(solution)/shard_map/finish/pallas_call | solution.py:1243

commit v6 on v5

--- a/solution.py
+++ b/solution.py
@@ -890,7 +890,7 @@
     mid[...] = middle
     normed, _ = norm_stats(middle)
     e2[net.slot] = (normed * vec[3:4, :] + vec[4:5, :]).astype(BF)
-    gather_e2 = Gather(net, e2, shard // 2)
+    gather_e2 = Gather(net, e2, shard * 3 // 4)
     gather_e2.start()
     weight_d.relay()
     gather_g.relay(1)

time: 167 us -> 167 us (level)
  no operation moved by 1% of the time
where the time goes in v6:
time: 167 us
  Pallas kernels  166 us (99%)
    pallas_call x1, Pallas kernels, layer_on_square(): pl.pallas_call(functools.partial(layer_kernel, EPS, MASKED, used), out_sh...  162 us
    pallas_call x1, Pallas kernels, layer_on_square(): pl.pallas_call(finish, grid=(steps,), out_shape=(sds((half_tokens, quarte...  4.74 us

profile of v6, /device:TPU:0, one launch (start us, length us, event | category | flops | bytes accessed | tf_op | source)
XLA Modules:
  0.0 167.3 jit_solution(15118468204150200684)
XLA Ops:
  0.7 161.7 %tree_layer.1 = (bf16[512,256]{1,0:T(8,128)(2,1)}, bf16[512,256]{1,0:T(8,128)(2,1)}, bf16[4,256,128]{2,1,0:T(8,128)(2,1)}, bf16[4,256,256]{2,1,0:T(8,128)(2,1)},...) custom-call(bf16[512,256]{1,0:T(8,128)(2,1)} %refs_0_.1, ...), custom_call_target="tpu_custom_call" | custom-call | tf_op jit(solution)/shard_map/tree_layer/pallas_call | solution.py:1191
  162.3 4.7 %finish.1 = (f32[512,256]{1,0:T(8,128)}, f32[512,256]{1,0:T(8,128)}, f32[3,256,512]{2,1,0:T(8,128)}, f32[512,256]{1,0:T(8,128)}, f32[2048,256]{1,0:T(8,128)}, /*...) custom-call(bf16[512,256]{1,0:T(8,128)(2,1)} %get-tuple-element.37.r, ...), custom_call_target="tpu_custom_call" | custom-call | tf_op jit(solution)/shard_map/finish/pallas_call | solution.py:1243
